TPU v7x, 32 devices: a whole 2x2x4 slice. The times are simulated.
32 devices in a mesh: gx: 4 (over z), gy: 2 (over x), gz: 4 (over y, core).
Axes of the slice: x: 2, y: 2, z: 4, core: 2. Of those that a mesh axis runs over, the one named last changes fastest.
Arguments:
- fine_rhs: float32 [96, 32, 1024], P(('gx', 'gy', 'gz')), may hold values from -6 to 6
- coarse_rhs: float32 [128, 64, 512], P('gx', 'gy', 'gz'), may hold values from -6 to 6
- patch_count: int32 [32], P(('gx', 'gy', 'gz')), may hold values from 2 to 3, as said below
- patch_corner: int32 [96, 3], P(('gx', 'gy', 'gz')), may hold values from 0 to 496, as said below
Outputs:
- fine_solution: float32 [96, 32, 1024], P(('gx', 'gy', 'gz'))
- coarse_solution: float32 [128, 64, 512], P('gx', 'gy', 'gz')
Inputs may be any that keep to these rules, and one draw needn't show every extreme that they name: Slots 0 to patch_count[d] - 1 of device d hold live patches, the others are unused. `patch_corner`: A live patch's footprint starts at a multiple of 16 in each dimension and lies inside the coarse block of one device with the same gx and gy indices as the patch's owner; live footprints never intersect; at most 2 live patches of one device lie in the block of any one device. Rows of unused slots are zero.
All inputs are finite; a program needn't handle non-finite values.
Results may differ from a plain program's by a relative error of at most 0.00007.
Values sent between devices are 32-bit elements; how exact they have to be, the bound alone decides.
No kernel may reach another device: no remote copies, remote signals or barrier semaphores. Data moves between devices by JAX's collectives and lax.ppermute only.
A program may use at most 64 MiB of HBM per device.

v0:
```python
import functools

import jax
import jax.numpy as jnp
from jax import lax
from jax.experimental import pallas as pl
from jax.experimental.pallas import tpu as pltpu
from jax.sharding import PartitionSpec as P

LANES = 128
SUB = 8
RIM = 3
CAP = 2
F32 = jnp.float32
BF16 = jnp.bfloat16


def iota(shape, dim):
    return lax.broadcasted_iota(jnp.int32, shape, dim)


def dot2(x, table):
    high = x.astype(BF16)
    low = (x - high.astype(F32)).astype(BF16)
    both = jnp.concatenate([high, low], 1)
    return jnp.dot(both, jnp.concatenate([table, table], 0), preferred_element_type=F32)


class Plan:
    def __init__(self, fine_shape, coarse_shape):
        self.slots, self.pe, self.merged = fine_shape
        self.foot = self.pe // 2
        self.cx, self.cy, self.cz = coarse_shape
        assert self.cz == LANES and self.merged == self.pe * self.pe
        assert self.foot * self.foot == 2 * LANES and self.pe * 4 == LANES
        self.tiles = self.merged // LANES
        self.fpitch = self.pe + SUB
        self.frows = SUB + self.slots * self.fpitch
        self.nx, self.ny, self.nz = (lax.axis_size(a) for a in ("gx", "gy", "gz"))
        self.pitch = self.cy + SUB
        self.crows = SUB + (self.cx + 2 * RIM) * self.pitch + SUB
        self.spots_y = self.cy // self.foot
        self.spots_z = self.cz // self.foot
        self.avg_rows = self.slots * 2 * self.foot
        self.zrows = self.cy
        assert self.cx * 4 == LANES
        self.erows = CAP * self.foot
        self.elanes = 3 * LANES
        self.win = self.foot + 2
        self.elow = self.win * self.win
        assert self.elow + 2 * self.foot <= self.elanes
        self.yrows = RIM * self.cx
        self.xrows = 3 * self.pitch + SUB
        assert self.xrows == LANES

    def row(self, x, y):
        return SUB + (x + RIM) * self.pitch + y

    def faces(self, shift):
        return shift == 1, shift == self.nz - 1

    def msg_rows(self, shift):
        high, low = self.faces(shift)
        return self.avg_rows + SUB + self.zrows * (int(high) + int(low))


def fine_neighbors(ref, t, row, tiles):
    lane = iota((SUB, LANES), 1)
    mid = ref[t, pl.ds(row, SUB), :]
    total = ref[t, pl.ds(row - 1, SUB), :] + ref[t, pl.ds(row + 1, SUB), :]
    total += jnp.where(lane % 32 == 0, 0.0, pltpu.roll(mid, 1, 1))
    total += jnp.where(lane % 32 == 31, 0.0, pltpu.roll(mid, LANES - 1, 1))
    before = ref[t - 1, pl.ds(row, SUB), :] if t else jnp.zeros_like(mid)
    after = ref[t + 1, pl.ds(row, SUB), :] if t + 1 < tiles else jnp.zeros_like(mid)
    total += pltpu.roll(jnp.where(lane >= LANES - 32, before, mid), 32, 1)
    total += pltpu.roll(jnp.where(lane < 32, after, mid), LANES - 32, 1)
    return mid, total


def zero_gaps(ref, plan):
    gap = jnp.zeros((SUB, LANES), F32)
    for t in range(plan.tiles):
        for p in range(plan.slots + 1):
            row = p * plan.fpitch
            if row + SUB <= plan.frows:
                ref[t, pl.ds(row, SUB), :] = gap


def pack_face(ref, plan, low):
    outs = []
    lane = iota((SUB, LANES), 1)
    start = 0 if low else plan.cz - RIM
    for j in range(plan.cy // SUB):
        acc = jnp.zeros((SUB, LANES), F32)
        for x in range(plan.cx):
            v = pltpu.roll(ref[pl.ds(x * plan.cy + j * SUB, SUB), :], (4 * x - start) % LANES, 1)
            acc = jnp.where(lane // 4 == x, v, acc)
        outs.append(acc)
    return outs


def patch_code(plan, count, corner_ref, p):
    spot_x = corner_ref[p, 0] % plan.cx // plan.foot
    spot_y = corner_ref[p, 1] % plan.cy // plan.foot
    spot_z = corner_ref[p, 2] // plan.foot
    code = (spot_x * plan.spots_y + spot_y) * (plan.spots_z * plan.nz) + spot_z
    return jnp.where(p < count, code, -1)


def pre_kernel(plan, count_ref, corner_hbm, fine_hbm, coarse_hbm, rhs, pre_ref, blk, *rest):
    msg_refs, (fine_ref, res, corner_ref, sems) = rest[:-4], rest[-4:]
    pe, foot, tiles = plan.pe, plan.foot, plan.tiles
    copies = [pltpu.make_async_copy(fine_hbm.at[p], fine_ref.at[p], sems.at[p]) for p in range(plan.slots)]
    at = plan.slots
    copies.append(pltpu.make_async_copy(coarse_hbm, blk, sems.at[at]))
    copies.append(pltpu.make_async_copy(corner_hbm, corner_ref, sems.at[at + 1]))
    for copy in copies:
        copy.start()
    zero_gaps(rhs, plan)
    zero_gaps(pre_ref, plan)
    source, target = iota((4 * LANES, LANES), 0), iota((4 * LANES, LANES), 1)
    place = (source // LANES) * 32 + (source % LANES) // 64 * 16 + source % 32 // 2
    table = jnp.where(place == target, 0.5, 0.0).astype(BF16)
    for p in range(plan.slots):
        copies[p].wait()
        start = SUB + p * plan.fpitch
        for j in range(pe // SUB):
            for t in range(tiles):
                rhs[t, pl.ds(start + j * SUB, SUB), :] = fine_ref[
                    p, pl.ds(j * SUB, SUB), t * LANES : (t + 1) * LANES
                ]
        for j in range(pe // SUB):
            for t in range(tiles):
                mid, total = fine_neighbors(rhs, t, start + j * SUB, tiles)
                pre_ref[t, pl.ds(start + j * SUB, SUB), :] = 0.165 * mid + 0.0225 * total
        for j in range(pe // SUB):
            for t in range(tiles):
                mid, total = fine_neighbors(pre_ref, t, start + j * SUB, tiles)
                rows = pl.ds(start + j * SUB, SUB)
                res[t, rows, :] = rhs[t, rows, :] - (6.0 * mid - total)
        lines = []
        for half in range(2):
            cols = []
            for k in range(4):
                t = 4 * half + k
                cols.append(
                    res[t, pl.ds(start, foot, stride=2), :]
                    + res[t, pl.ds(start + 1, foot, stride=2), :]
                )
            lines.append(jnp.concatenate(cols, 1))
        value = dot2(jnp.concatenate(lines, 0), table)
        for ref in msg_refs:
            ref[pl.ds(p * 2 * foot, 2 * foot), :] = value
    for copy in copies[at:]:
        copy.wait()
    lane = iota((SUB, LANES), 1)
    tags = jnp.zeros((SUB, LANES), F32)
    for p in range(plan.slots):
        code = patch_code(plan, count_ref[0], corner_ref, p)
        tags = jnp.where(lane == p, code.astype(F32), tags)
    packed = {}
    for shift, ref in enumerate(msg_refs, 1):
        at = plan.avg_rows
        ref[pl.ds(at, SUB), :] = tags
        at += SUB
        for low, wanted in enumerate(plan.faces(shift)):
            if wanted:
                if low not in packed:
                    packed[low] = pack_face(blk, plan, low)
                for j, v in enumerate(packed[low]):
                    ref[pl.ds(at + j * SUB, SUB), :] = v
                at += plan.zrows


def decode(plan, code):
    total_z = plan.spots_z * plan.nz
    spot_z = code % total_z
    spot = code // total_z
    return (
        spot // plan.spots_y * plan.foot,
        spot % plan.spots_y * plan.foot,
        spot_z // plan.spots_z,
        spot_z * plan.foot,
    )


def message_code(plan, ref, p):
    return ref[plan.avg_rows, p].astype(jnp.int32)


def place_patch(plan, ref, base, code, comp, block=True, rims=True):
    me = lax.axis_index("gz")
    x0, y0, home, z0 = decode(plan, code)
    dz = z0 - me * plan.cz

    inside = (dz >= 0) & (dz < plan.cz)
    wanted = (code >= 0) & (dz >= -plan.foot) & (dz <= plan.cz)
    if not rims:
        wanted = wanted & inside
    if not block:
        wanted = wanted & jnp.logical_not(inside)

    @pl.when(wanted)
    def _():
        offset = jnp.where(inside, 0, plan.crows)
        lane0 = (dz + plan.cz) % plan.cz
        lane = iota((plan.foot, LANES), 1)
        window = (lane >= lane0) & (lane < lane0 + plan.foot)
        first = offset + plan.row(x0, y0)
        for y in range(plan.foot):
            half, k = divmod(y * plan.foot, LANES)
            v = ref[pl.ds(base + half * plan.foot, plan.foot), :]
            v = pltpu.roll(v, (lane0 + LANES - k) % LANES, 1)
            rows = pl.ds(first + y, plan.foot, stride=plan.pitch)
            comp[rows, :] = jnp.where(window, v, comp[rows, :])


def flags(axis, size):
    index = lax.axis_index(axis)
    return index > 0, index < size - 1


def fixed_kernel(plan, rhs, pre_ref, out, work):
    zero_gaps(work, plan)
    for source, target in ((pre_ref, work), (work, out)):

        def rows8(i, carry):
            p, j = i // (plan.pe // SUB), i % (plan.pe // SUB)
            row = pl.multiple_of(SUB + p * plan.fpitch + j * SUB, SUB)
            for t in range(plan.tiles):
                mid, total = fine_neighbors(source, t, row, plan.tiles)
                rows = pl.ds(row, SUB)
                target[t, rows, :] = 0.1 * mid + 0.15 * (rhs[t, rows, :] + total)
            return carry

        lax.fori_loop(0, plan.slots * (plan.pe // SUB), rows8, 0)


def base_kernel(plan, blk, own_ref, comp):
    cx, cy = plan.cx, plan.cy
    end = SUB + RIM * plan.pitch
    for base in (0, plan.crows):
        comp[pl.ds(base, end), :] = jnp.zeros((end, LANES), F32)
        comp[pl.ds(base + plan.crows - end, end), :] = jnp.zeros((end, LANES), F32)
        for x in range(cx):
            comp[pl.ds(base + plan.row(x, cy), SUB), :] = jnp.zeros((SUB, LANES), F32)
    for x in range(cx):
        comp[pl.ds(plan.row(x, 0), cy), :] = blk[pl.ds(x * cy, cy), :]
        comp[pl.ds(plan.crows + plan.row(x, 0), cy), :] = jnp.zeros((cy, LANES), F32)
    for p in range(plan.slots):
        place_patch(plan, own_ref, p * 2 * plan.foot, message_code(plan, own_ref, p), comp, rims=False)


def compose_kernel(plan, n_y, comp_in, own_ref, *rest):
    msg_refs, (comp, *y_sends) = rest[: plan.nz - 1], rest[plan.nz - 1 :]
    del comp_in
    cx, cy = plan.cx, plan.cy
    lane = iota((SUB, LANES), 1)
    zero = jnp.zeros((SUB, LANES), F32)
    lo_face, hi_face = [zero] * (cy // SUB), [zero] * (cy // SUB)
    has_lo, has_hi = flags("gz", plan.nz)
    for shift, ref in enumerate(msg_refs, 1):
        at = plan.avg_rows + SUB
        for low, wanted in enumerate(plan.faces(shift)):
            if wanted:
                got = [ref[pl.ds(at + j * SUB, SUB), :] for j in range(cy // SUB)]
                if low:
                    hi_face = [jnp.where(has_hi, v, 0.0) for v in got]
                else:
                    lo_face = [jnp.where(has_lo, v, 0.0) for v in got]
                at += plan.zrows
    for x in range(cx):
        for j in range(cy // SUB):
            rows = pl.ds(plan.crows + plan.row(x, j * SUB), SUB)
            lo = pltpu.roll(lo_face[j], (plan.cz - RIM - 4 * x) % LANES, 1)
            hi = pltpu.roll(hi_face[j], (-4 * x) % LANES, 1)
            v = jnp.where(lane < RIM, hi, comp[rows, :])
            comp[rows, :] = jnp.where(lane >= plan.cz - RIM, lo, v)
    for p in range(plan.slots):
        for ref in (own_ref, *msg_refs):
            code = message_code(plan, ref, p)
            place_patch(plan, ref, p * 2 * plan.foot, code, comp, block=ref is not own_ref)
    odd = lax.axis_index("gy") % 2
    for start, ref in enumerate(y_sends):
        y0 = jnp.where(odd == start, cy - RIM, 0)
        rims = []
        for k in range(RIM):
            ref[pl.ds(k * cx, cx), :] = comp[pl.ds(plan.row(0, y0 + k), cx, stride=plan.pitch), :]
            v = comp[pl.ds(plan.crows + plan.row(0, y0 + k), cx, stride=plan.pitch), :]
            rims += [v[j * SUB : (j + 1) * SUB] for j in range(cx // SUB)]
        ref[pl.ds(RIM * cx, SUB), :] = pack_rims(rims)


def pack_rims(rims):
    lane = iota((SUB, LANES), 1)
    acc = jnp.zeros((SUB, LANES), F32)
    for i, v in enumerate(rims):
        acc = jnp.where(lane // SUB == i, pltpu.roll(v, (SUB * i + 4) % LANES, 1), acc)
    return acc


def unpack_rim(packed, i):
    lane = iota((SUB, LANES), 1)
    v = pltpu.roll(packed, (-(SUB * i + 4)) % LANES, 1)
    return jnp.where((lane < RIM) | (lane >= LANES - RIM), v, 0.0)


def put_yface(plan, msg, comp, y):
    for k in range(RIM):
        comp[pl.ds(plan.row(0, y + k), plan.cx, stride=plan.pitch), :] = msg[pl.ds(k * plan.cx, plan.cx), :]
        packed = msg[pl.ds(RIM * plan.cx, SUB), :]
        n = plan.cx // SUB
        rims = jnp.concatenate([unpack_rim(packed, k * n + j) for j in range(n)], 0)
        comp[pl.ds(plan.crows + plan.row(0, y + k), plan.cx, stride=plan.pitch), :] = rims


def xface_kernel(plan, n_y, n_x, comp_in, second_in, *rest):
    y_refs, (comp, second, *x_sends) = rest[:n_y], rest[n_y:]
    del comp_in, second_in, second
    put_yfaces(plan, y_refs, comp)
    odd = lax.axis_index("gx") % 2
    for start, ref in enumerate(x_sends):
        first = pl.multiple_of(plan.row(jnp.where(odd == start, plan.cx - RIM, 0), 0) - SUB, SUB)
        ref[pl.ds(0, plan.xrows), :] = comp[pl.ds(first, plan.xrows), :]
        rims = [
            comp[pl.ds(plan.crows + first + i * SUB, SUB), :] for i in range(plan.xrows // SUB)
        ]
        ref[pl.ds(plan.xrows, SUB), :] = pack_rims(rims)


def put_yfaces(plan, y_refs, comp):
    odd = lax.axis_index("gy") % 2
    for i, ref in enumerate(y_refs):
        at_high = (odd == 0) if i == 0 else (odd == 1)
        put_yface(plan, ref, comp, jnp.where(at_high, plan.cy, -RIM))


def put_xfaces(plan, x_refs, comp):
    odd = lax.axis_index("gx") % 2
    for i, ref in enumerate(x_refs):
        at_high = (odd == 0) if i == 0 else (odd == 1)
        first = plan.row(jnp.where(at_high, plan.cx, -RIM), 0) - SUB
        packed = ref[pl.ds(plan.xrows, SUB), :]
        row = iota((SUB, LANES), 0)
        n = plan.xrows // SUB
        for k in range(n):
            for tile in range(2):
                v = ref[pl.ds(k * SUB, SUB), :] if tile == 0 else unpack_rim(packed, k)
                rows = pl.ds(tile * plan.crows + first + k * SUB, SUB)
                if k == 0:
                    v = jnp.where(row >= SUB - RIM, v, comp[rows, :])
                if k == n - 1:
                    v = jnp.where(row < RIM, v, comp[rows, :])
                comp[rows, :] = v


class Sweeps:
    def __init__(self, plan, comp, second, third=None):
        self.plan, self.comp, self.second, self.third = plan, comp, second, third
        self.lane, row = iota((SUB, LANES), 1), iota((SUB, LANES), 0)
        z_lo, z_hi = flags("gz", plan.nz)
        y_lo, y_hi = flags("gy", plan.ny)
        lane = self.lane
        self.zmask = jnp.where(((lane >= LANES - RIM) & z_lo) | ((lane < RIM) & z_hi), 1.0, 0.0)
        self.ymask = jnp.where(((row >= SUB - RIM) & y_lo) | ((row < RIM) & y_hi), 1.0, 0.0)
        self.main = plan.cy // SUB

    def at(self, x, j):
        return pl.multiple_of(self.plan.row(x, j * SUB), SUB)

    def stencil(self, ref, at):
        crows, pitch, lane = self.plan.crows, self.plan.pitch, self.lane
        mids, sums = [], []
        for base in (0, crows):
            mids.append(ref[pl.ds(base + at, SUB), :])
            total = ref[pl.ds(base + at - 1, SUB), :] + ref[pl.ds(base + at + 1, SUB), :]
            total += ref[pl.ds(base + at - pitch, SUB), :] + ref[pl.ds(base + at + pitch, SUB), :]
            sums.append(total)
        for i in range(2):
            sums[i] += pltpu.roll(jnp.where(lane == LANES - 1, mids[1 - i], mids[i]), 1, 1)
            sums[i] += pltpu.roll(jnp.where(lane == 0, mids[1 - i], mids[i]), LANES - 1, 1)
        return mids, sums

    def step2(self, x, j):
        at = self.at(x, j)
        mids, sums = self.stencil(self.comp, at)
        for i in range(2):
            v = 0.165 * mids[i] + 0.0225 * sums[i]
            v = v * self.ymask if j == self.main else v
            self.second[pl.ds(i * self.plan.crows + at, SUB), :] = v * self.zmask if i else v

    def step3(self, x, j):
        at, crows, lane = self.at(x, j), self.plan.crows, self.lane
        mids, sums = self.stencil(self.second, at)
        outs = []
        for i in range(2):
            v = 0.1 * mids[i] + 0.15 * (self.comp[pl.ds(i * crows + at, SUB), :] + sums[i])
            v = v * self.ymask if j == self.main else v
            outs.append(v * self.zmask if i else v)
        self.third[pl.ds(at, SUB), :] = outs[0]
        self.third[pl.ds(crows + at, SUB), :] = jnp.where(lane >= LANES - 2, outs[1], outs[0])
        self.third[pl.ds(2 * crows + at, SUB), :] = jnp.where(lane < 2, outs[1], outs[0])

    def planes(self, step, first, last, tiles, unroll=2):
        def body(x, carry):
            for j in tiles:
                step(x, j)
            return carry

        lax.fori_loop(first, last + 1, body, 0, unroll=unroll)


def inner_kernel(plan, comp, second):
    s = Sweeps(plan, comp, second)
    s.planes(s.step2, 1, plan.cx - 2, range(1, s.main - 1), unroll=3)


def middle_kernel(plan, comp, second_in, second, third):
    del second_in
    s = Sweeps(plan, comp, second, third)
    s.step2(0, s.main)
    s.planes(s.step2, 1, plan.cx - 2, (0, s.main - 1, s.main))
    s.planes(s.step3, 2, plan.cx - 3, range(s.main + 1))


def put_xfaces(plan, x_refs, comp):
    odd = lax.axis_index("gx") % 2
    for i, ref in enumerate(x_refs):
        at_high = (odd == 0) if i == 0 else (odd == 1)
        first = pl.multiple_of(plan.row(jnp.where(at_high, plan.cx, -RIM), 0) - SUB, SUB)
        packed = ref[pl.ds(plan.xrows, SUB), :]
        row = iota((SUB, LANES), 0)
        n = plan.xrows // SUB
        for k in range(n):
            for tile in range(2):
                v = ref[pl.ds(k * SUB, SUB), :] if tile == 0 else unpack_rim(packed, k)
                rows = pl.ds(tile * plan.crows + first + k * SUB, SUB)
                if k == 0:
                    v = jnp.where(row >= SUB - RIM, v, comp[rows, :])
                if k == n - 1:
                    v = jnp.where(row < RIM, v, comp[rows, :])
                comp[rows, :] = v


def edge_kernel(plan, n_x, comp_in, second_in, third_in, own_ref, *rest):
    x_refs, msg_refs = rest[:n_x], rest[n_x : n_x + plan.nz - 1]
    comp, second, third, *e_refs = rest[n_x + plan.nz - 1 :]
    del comp_in, second_in, third_in
    cx, pitch, crows = plan.cx, plan.pitch, plan.crows
    put_xfaces(plan, x_refs, comp)
    s = Sweeps(plan, comp, second, third)
    x_lo, x_hi = flags("gx", plan.nx)
    every = range(s.main + 1)
    s.step2(-RIM, s.main)
    s.step2(cx - 2, s.main)
    for x in (-2, -1, 0, cx - 1, cx, cx + 1):
        for j in every:
            s.step2(x, j)
    for has, x in ((x_lo, 1 - RIM), (x_hi, cx)):

        @pl.when(jnp.logical_not(has))
        def _():
            for base in (0, crows):
                second[pl.ds(base + plan.row(x, -RIM), 2 * pitch), :] = jnp.zeros((2 * pitch, LANES), F32)

    s.step3(1 - RIM, s.main)
    s.step3(cx - 3, s.main)
    for x in (-1, 0, 1, cx - 2, cx - 1, cx):
        for j in every:
            s.step3(x, j)
    for has, x in ((x_lo, -1), (x_hi, cx)):

        @pl.when(jnp.logical_not(has))
        def _():
            for base in (0, crows, 2 * crows):
                third[pl.ds(base + plan.row(x, -RIM), pitch), :] = jnp.zeros((pitch, LANES), F32)

    me = lax.axis_index("gz")
    for shift in range(plan.nz):
        tags = msg_refs[plan.nz - shift - 1] if shift else own_ref
        used = 0
        for p in range(plan.slots):
            code = message_code(plan, tags, p)
            x0, y0, home, z0 = decode(plan, code)
            here = (code >= 0) & (home == me)

            @pl.when(here)
            def _():
                cut_patch(
                    plan, third, e_refs[shift], jnp.minimum(used, CAP - 1) * plan.foot, x0, y0, z0 % plan.cz
                )

            used = used + here.astype(jnp.int32)


def cut_patch(plan, third, out, base, x0, y0, z0):
    foot, pitch, crows, win = plan.foot, plan.pitch, plan.crows, plan.win
    base = pl.multiple_of(base, SUB)
    lane = iota((foot, LANES), 1)
    offset = jnp.where(z0 == 0, crows, jnp.where(z0 == plan.cz - foot, 2 * crows, 0))
    outs = [jnp.zeros((foot, LANES), F32) for _ in range(plan.elanes // LANES)]

    def put(v, source, target, width):
        tile, k = divmod(target, LANES)
        v = pltpu.roll(v, (k - source + 2 * LANES) % LANES, 1)
        outs[tile] = jnp.where((lane >= k) & (lane < k + width), v, outs[tile])
        if k + width > LANES:
            outs[tile + 1] = jnp.where(lane < k + width - LANES, v, outs[tile + 1])

    for y in range(-1, foot + 1):
        v = third[pl.ds(offset + plan.row(x0, y0 + y), foot, stride=pitch), :]
        put(v, z0 - 1, (y + 1) * win, win)
    for i, x in enumerate((-1, foot)):
        v = third[pl.ds(pl.multiple_of(plan.row(x0 + x, y0), SUB), foot), :]
        put(v, z0, plan.elow + i * foot, foot)
    for i, v in enumerate(outs):
        out[pl.ds(base, foot), i * LANES : (i + 1) * LANES] = v


def emit_kernel(plan, third, out_ref):
    for x in range(plan.cx):
        out_ref[pl.ds(x * plan.cy, plan.cy), :] = third[pl.ds(plan.row(x, 0), plan.cy), :]


def post_kernel(plan, own_ref, fixed, *rest):
    e_refs, (out_hbm, out_ref, ups, first, ghost, yghost, sems) = rest[: plan.nz], rest[plan.nz :]
    pe, foot, tiles, slots, win = plan.pe, plan.foot, plan.tiles, plan.slots, plan.win
    me = lax.axis_index("gz")
    codes = [message_code(plan, own_ref, p) for p in range(slots)]
    homes = [decode(plan, c)[2] for c in codes]
    cuts = []
    for p in range(slots):
        rank = 0
        for q in range(p):
            rank = rank + ((homes[q] == homes[p]) & (codes[q] >= 0)).astype(jnp.int32)
        rank = jnp.minimum(rank, CAP - 1)
        shift = (me - homes[p] + plan.nz) % plan.nz
        got = [jnp.zeros((foot, LANES), F32)] * 3
        for s in range(plan.nz):
            rows = pl.ds(pl.multiple_of(rank * foot, SUB), foot)
            take = (shift == s) & (codes[p] >= 0)
            got = [
                jnp.where(take, e_refs[s][rows, i * LANES : (i + 1) * LANES], g)
                for i, g in enumerate(got)
            ]
        cuts.append(got)
    lane16 = iota((foot, LANES), 1)

    def lanes_from(got, at):
        tile, k = divmod(at, LANES)
        v = pltpu.roll(got[tile], (LANES - k) % LANES, 1)
        if k and tile + 1 < len(got):
            v = jnp.where(lane16 < LANES - k, v, pltpu.roll(got[tile + 1], LANES - k, 1))
        return v

    source, target = iota((LANES, LANES), 0), iota((LANES, LANES), 1)
    q, fz = target // 32, target % 32
    a = 1 + q // 2
    own_lane = a * win + fz // 2 + 1
    side_y = own_lane + jnp.where(q % 2 == 0, -win, win)
    side_z = own_lane + jnp.where(fz % 2 == 0, -1, 1)
    up = jnp.where(source == own_lane, 1.0, 0.0)
    around = 3.0 * up + jnp.where(source == side_y, 1.0, 0.0) + jnp.where(source == side_z, 1.0, 0.0)
    zface = jnp.where((source == side_z) & ((fz == 0) | (fz == pe - 1)), 1.0, 0.0)
    table = jnp.concatenate([up, around, zface], 1).astype(BF16)
    work = [lanes_from(got, 2 * t * win) for got in cuts for t in range(tiles)]
    spread = dot2(jnp.concatenate(work, 0), table)
    low_y = jnp.where((target >= LANES - 32) & (source == fz // 2 + 1), 1.0, 0.0)
    high_y = jnp.where((target < 32) & (source == 3 * win + fz // 2 + 1), 1.0, 0.0)
    ends = [lanes_from(got, 0) for got in cuts], [lanes_from(got, 2 * (tiles - 1) * win) for got in cuts]
    lows = dot2(jnp.concatenate(ends[0], 0), low_y.astype(BF16))
    highs = dot2(jnp.concatenate(ends[1], 0), high_y.astype(BF16))
    xsel = jnp.where((source == fz // 2), 1.0, 0.0).astype(BF16)
    xfaces = dot2(
        jnp.concatenate([lanes_from(got, plan.elow + i * foot) for got in cuts for i in range(2)], 0), xsel
    )
    lane1 = iota((1, LANES), 1)
    copies = [pltpu.make_async_copy(out_ref.at[p], out_hbm.at[p], sems.at[p]) for p in range(slots)]
    lane = iota((SUB, LANES), 1)
    for p in range(slots):
        start = SUB + p * plan.fpitch
        ustart = SUB + p * (foot + SUB)
        for i, (v, k) in enumerate(((lows, 0), (highs, 1))):
            line = v[p * foot : (p + 1) * foot]
            for parity in range(2):
                yghost[k, pl.ds(start + parity, foot, stride=2), :] = line
        for t in range(tiles):
            block = spread[(p * tiles + t) * foot : (p * tiles + t + 1) * foot]
            mine = block[:, 0:LANES]
            ups[t, pl.ds(ustart, foot), :] = mine
            for i, (urow, row) in enumerate(((ustart - 1, start - 1), (ustart + foot, start + pe))):
                face = xfaces[(2 * p + i) * foot : (2 * p + i + 1) * foot]
                line = jnp.where(lane1 < 64, face[2 * t : 2 * t + 1], face[2 * t + 1 : 2 * t + 2])
                ups[t, pl.ds(urow, 1), :] = line
                first[t, pl.ds(row, 1), :] = line
            base = 0.1 * mine + 0.15 * block[:, LANES : 2 * LANES]
            for parity, shift in enumerate((-1, 1)):
                value = base + 0.15 * ups[t, pl.ds(ustart + shift, foot), :]
                first[t, pl.ds(start + parity, foot, stride=2), :] = value
                ghost[t, pl.ds(start + parity, foot, stride=2), :] = block[:, 2 * LANES :]
        alive = codes[p] >= 0
        for j in range(pe // SUB):
            rows = pl.ds(start + j * SUB, SUB)
            for t in range(tiles):
                mid = first[t, rows, :]
                side = ghost[t, rows, :]
                total = first[t, pl.ds(start + j * SUB - 1, SUB), :] + first[t, pl.ds(start + j * SUB + 1, SUB), :]
                total += jnp.where(lane % 32 == 0, side, pltpu.roll(mid, 1, 1))
                total += jnp.where(lane % 32 == 31, side, pltpu.roll(mid, LANES - 1, 1))
                before = first[t - 1, rows, :] if t else yghost[0, rows, :]
                after = first[t + 1, rows, :] if t + 1 < tiles else yghost[1, rows, :]
                total += pltpu.roll(jnp.where(lane >= LANES - 32, before, mid), 32, 1)
                total += pltpu.roll(jnp.where(lane < 32, after, mid), LANES - 32, 1)
                value = fixed[t, rows, :] + (0.1 * mid + 0.15 * total)
                out_ref[p, pl.ds(j * SUB, SUB), t * LANES : (t + 1) * LANES] = jnp.where(alive, value, 0.0)
        copies[p].start()
    for copy in copies:
        copy.wait()


VMEM = pl.BlockSpec(memory_space=pltpu.VMEM)
HBM = pl.BlockSpec(memory_space=pltpu.HBM)
SMEM = pl.BlockSpec(memory_space=pltpu.SMEM)


def call(kernel, name, outs, args, scratch=(), aliases=None, smem=0, hbm_in=0, hbm_out=0, sems=0, cost=0):
    spaces = [s if isinstance(s, pl.MemoryRef) else pltpu.VMEM(s, F32) for s in scratch]
    return pl.pallas_call(
        kernel,
        name=name,
        out_shape=[jax.ShapeDtypeStruct(s, F32) for s in outs],
        in_specs=[SMEM] * smem + [HBM] * hbm_in + [VMEM] * (len(args) - hbm_in - smem),
        out_specs=[HBM] * hbm_out + [VMEM] * (len(outs) - hbm_out),
        scratch_shapes=spaces + ([pltpu.SemaphoreType.DMA((sems,))] if sems else []),
        input_output_aliases=aliases or {},
        cost_estimate=pl.CostEstimate(flops=cost, bytes_accessed=cost, transcendentals=0) if cost else None,
        compiler_params=pltpu.CompilerParams(vmem_limit_bytes=16 << 20),
    )(*args)


def swap_pairs(axis, size, sends):
    got = []
    for start, send in enumerate(sends):
        pairs = [(i, i + 1) for i in range(start, size - 1, 2)]
        got.append(lax.ppermute(send, axis, pairs + [(b, a) for a, b in pairs]))
    return got


def per_device(fine_rhs, coarse_rhs, patch_count, patch_corner):
    plan = Plan(fine_rhs.shape, coarse_rhs.shape)
    fine_shape = (plan.tiles, plan.frows, LANES)
    block_shape = (plan.cx * plan.cy, plan.cz)
    comp_shape = (2 * plan.crows, LANES)
    third_shape = (3 * plan.crows, LANES)
    yshape, xshape = (plan.yrows + SUB, LANES), (plan.xrows + SUB, LANES)
    eshape = (plan.erows, plan.elanes)
    n_y, n_x = min(plan.ny - 1, 2), min(plan.nx - 1, 2)
    shifts = range(1, plan.nz)
    bind = functools.partial
    rhs, pre, block, *sends = call(
        bind(pre_kernel, plan),
        "pre",
        [fine_shape, fine_shape, block_shape] + [(plan.msg_rows(s), LANES) for s in shifts],
        [patch_count]
        + [
            pltpu.with_memory_space_constraint(a, pltpu.HBM)
            for a in (patch_corner, fine_rhs, coarse_rhs.reshape(block_shape))
        ],
        scratch=(fine_rhs.shape, fine_shape, pltpu.VMEM(patch_corner.shape, jnp.int32)),
        smem=1,
        hbm_in=3,
        sems=plan.slots + 2,
    )
    own = sends[0]

    def ring(s):
        return [(i, (i + s) % plan.nz) for i in range(plan.nz)]

    msgs = [lax.ppermute(m, "gz", ring(s)) for s, m in zip(shifts, sends)]
    (comp,) = call(bind(base_kernel, plan), "base", [comp_shape], (block, own), cost=4 << 20)
    (fixed,) = call(
        bind(fixed_kernel, plan), "fixed", [fine_shape], (rhs, pre), scratch=(fine_shape,), cost=4 << 20
    )
    comp, *ysends = call(
        bind(compose_kernel, plan, n_y), "compose", [comp_shape] + [yshape] * n_y, (comp, own, *msgs), aliases={0: 0}
    )
    ygot = swap_pairs("gy", plan.ny, ysends)
    (second,) = call(bind(inner_kernel, plan), "inner", [comp_shape], (comp,), cost=4 << 20)
    comp, second, *xsends = call(
        bind(xface_kernel, plan, n_y, n_x),
        "xface",
        [comp_shape, comp_shape] + [xshape] * n_x,
        (comp, second, *ygot),
        aliases={0: 0, 1: 1},
    )
    xgot = swap_pairs("gx", plan.nx, xsends)
    second, third = call(
        bind(middle_kernel, plan), "middle", [comp_shape, third_shape], (comp, second), aliases={1: 0}, cost=8 << 20
    )
    _, _, third, *cuts = call(
        bind(edge_kernel, plan, n_x),
        "edge",
        [comp_shape, comp_shape, third_shape] + [eshape] * plan.nz,
        (comp, second, third, own, *xgot, *msgs),
        aliases={0: 0, 1: 1, 2: 2},
    )
    back = [cuts[0]] + [lax.ppermute(cuts[s], "gz", ring(s)) for s in shifts]
    (out,) = call(bind(emit_kernel, plan), "emit", [block_shape], (third,), cost=2 << 20)
    (fine,) = call(
        bind(post_kernel, plan),
        "post",
        [fine_rhs.shape],
        (own, fixed, *back),
        scratch=(
            fine_rhs.shape,
            (plan.tiles, SUB + plan.slots * (plan.foot + SUB), LANES),
            fine_shape,
            fine_shape,
            (2, plan.frows, LANES),
        ),
        hbm_out=1,
        sems=plan.slots,
    )
    return fine, out.reshape(coarse_rhs.shape)


def solution(mesh):
    return jax.shard_map(
        per_device,
        mesh=mesh,
        in_specs=(
            P(("gx", "gy", "gz"), None, None),
            P("gx", "gy", "gz"),
            P(("gx", "gy", "gz")),
            P(("gx", "gy", "gz"), None),
        ),
        out_specs=(P(("gx", "gy", "gz"), None, None), P("gx", "gy", "gz")),
        check_vma=False,
    )
```

profile of v0, /device:TPU:10, one launch (start us, length us, event | category | flops | bytes accessed | tf_op | source)
XLA Modules:
  0.0 34.3 jit_solution(13975393170049822679)
XLA Ops:
  1.3 2.8 %pre.1 = (f32[8,128,128]{2,1,0:T(8,128)S(1)}, f32[8,128,128]{2,1,0:T(8,128)S(1)}, f32[1024,128]{1,0:T(8,128)S(1)}, f32[136,128]{1,0:T(8,128)S(1)}, f32[104,128]{1,0:T(8,128)S(1)}, /*index=5*/f32[136,128]{1,0:T(8,128)S(1)}) custom-call(s32[1]{0:T(128)S(6)} %copy.20.count_ref, s32[3,3]{1,0:T(4,128)} %corner_hbm.1, f32[3,32,1024]{2,1,0:T(8,128)} %fine_hbm.1, ...), custom_call_target="tpu_custom_call" | custom-call | tf_op jit(solution)/shard_map/pre/pallas_call | solution.py:628
  4.1 1.0 %collective-permute-start.2 = (f32[136,128]{1,0:T(8,128)S(1)}, f32[136,128]{1,0:T(8,128)S(1)}, u32[]{:S(2)}, u32[]{:S(2)}) collective-permute-start(f32[136,128]{1,0:T(8,128)S(1)} %get-tuple-element.26), channel_id=1, source_target_pairs={{0,3},{1,0},{2,1},{3,2},{4,7},{5,4},{6,5},{7,6},{8,11},{9,8},{10,9... | collective-permute-start | bytes 208904 | tf_op jit(solution)/shard_map/ppermute | solution.py:679
  5.1 0.0 collective-permute-start
  5.1 1.1 %collective-permute-start.1 = (f32[104,128]{1,0:T(8,128)S(1)}, f32[104,128]{1,0:T(8,128)S(1)}, u32[]{:S(2)}, u32[]{:S(2)}) collective-permute-start(f32[104,128]{1,0:T(8,128)S(1)} %get-tuple-element.25), channel_id=1, source_target_pairs={{0,2},{1,3},{2,0},{3,1},{4,6},{5,7},{6,4},{7,5},{8,10},{9,11},{10,... | collective-permute-start | bytes 159752 | tf_op jit(solution)/shard_map/ppermute | solution.py:679
  6.2 0.6 %base.1.comp_in = f32[3072,128]{1,0:T(8,128)S(1)} custom-call(f32[1024,128]{1,0:T(8,128)S(1)} %get-tuple-element.24.blk, f32[136,128]{1,0:T(8,128)S(1)} %get-tuple-element.21.own_ref), custom_call_target="tpu_custom_call" | custom-call | flops 4194304 | bytes 4194304 | tf_op jit(solution)/shard_map/base/pallas_call | solution.py:628
  6.8 3.0 %collective-permute-done.1.rest_1_.rest_3_ = f32[104,128]{1,0:T(8,128)S(1)} collective-permute-done((f32[104,128]{1,0:T(8,128)S(1)}, f32[104,128]{1,0:T(8,128)S(1)}, u32[]{:S(2)}, u32[]{:S(2)}) %collective-permute-start.1) | collective-permute-done | bytes 53280 | tf_op jit(solution)/shard_map/ppermute | solution.py:679
  9.8 0.0 collective-permute-done.2.rest_2_.rest_4_
  9.8 0.0 collective-permute-done.rest_0_.rest_2_
  9.8 2.2 %compose.1 = (f32[3072,128]{1,0:T(8,128)S(1)}, f32[104,128]{1,0:T(8,128)S(1)}) custom-call(f32[3072,128]{1,0:T(8,128)S(1)} %base.1.comp_in, f32[136,128]{1,0:T(8,128)S(1)} %get-tuple-element.21.own_ref, f32[136,128]{1,0:T(8,128)S(1)} %collective-permute-done.rest_0_.rest_2_, ...), custom_call_target="tpu_custom_call", output_to_operand_aliasing={{0}: (0, {})} | custom-call | tf_op jit(solution)/shard_map/compose/pallas_call | solution.py:628
  12.1 0.3 collective-permute-start.3
  12.3 1.0 %inner.1.second_in = f32[3072,128]{1,0:T(8,128)S(1)} custom-call(f32[3072,128]{1,0:T(8,128)S(1)} %get-tuple-element.27.comp.comp_in), custom_call_target="tpu_custom_call" | custom-call | flops 4194304 | bytes 4194304 | tf_op jit(solution)/shard_map/inner/pallas_call | solution.py:628
  13.3 3.0 %collective-permute-done.3.rest_0_ = f32[104,128]{1,0:T(8,128)S(1)} collective-permute-done((f32[104,128]{1,0:T(8,128)S(1)}, f32[104,128]{1,0:T(8,128)S(1)}, u32[]{:S(2)}, u32[]{:S(2)}) %collective-permute-start.3) | collective-permute-done | bytes 53280 | tf_op jit(solution)/shard_map/ppermute | solution.py:645
  16.3 0.2 xface.1
  16.4 0.5 %collective-permute-start.4 = (f32[136,128]{1,0:T(8,128)S(1)}, f32[136,128]{1,0:T(8,128)S(1)}, u32[]{:S(2)}, u32[]{:S(2)}) collective-permute-start(f32[136,128]{1,0:T(8,128)S(1)} %get-tuple-element.33), channel_id=1, source_target_pairs={{0,8},{16,24},{8,0},{24,16},{1,9},{17,25},{9,1},{25,17},{2,10},{18... | collective-permute-start | bytes 208904 | tf_op jit(solution)/shard_map/ppermute | solution.py:645
  16.9 4.3 %collective-permute-start.5 = (f32[136,128]{1,0:T(8,128)S(1)}, f32[136,128]{1,0:T(8,128)S(1)}, u32[]{:S(2)}, u32[]{:S(2)}) collective-permute-start(f32[136,128]{1,0:T(8,128)S(1)} %get-tuple-element.34), channel_id=1, source_target_pairs={{8,16},{16,8},{9,17},{17,9},{10,18},{18,10},{11,19},{19,11},{12,20... | collective-permute-start | bytes 208904 | tf_op jit(solution)/shard_map/ppermute | solution.py:645
  21.3 3.2 %middle.1 = (f32[3072,128]{1,0:T(8,128)S(1)}, f32[4608,128]{1,0:T(8,128)S(1)}) custom-call(f32[3072,128]{1,0:T(8,128)S(1)} %get-tuple-element.29.comp.comp_in, f32[3072,128]{1,0:T(8,128)S(1)} %get-tuple-element.30.second_in), custom_call_target="tpu_custom_call", output_to_operand_aliasing={{0}: (1, {})} | custom-call | flops 8388608 | bytes 8388608 | tf_op jit(solution)/shard_map/middle/pallas_call | solution.py:628
  24.5 0.0 collective-permute-done.4.rest_0_
  24.5 2.7 %edge.1 = (f32[3072,128]{1,0:T(8,128)S(1)}, f32[3072,128]{1,0:T(8,128)S(1)}, f32[4608,128]{1,0:T(8,128)S(1)}, f32[32,384]{1,0:T(8,128)S(1)}, f32[32,384]{1,0:T(8...) custom-call(f32[3072,128]{1,0:T(8,128)S(1)} %get-tuple-element.29.co, ...), custom_call_target="tpu_custom_call", output_to_operand_aliasing={{0}: (0, {}), {1}: (1, {}), {2}: (2, {})} | custom-call | tf_op jit(solution)/shard_map/edge/pallas_call | solution.py:628
  27.2 0.1 collective-permute-start.6
  27.3 0.4 %collective-permute-start.7 = (f32[32,384]{1,0:T(8,128)S(1)}, f32[32,384]{1,0:T(8,128)S(1)}, u32[]{:S(2)}, u32[]{:S(2)}) collective-permute-start(f32[32,384]{1,0:T(8,128)S(1)} %get-tuple-element.37), channel_id=1, source_target_pairs={{0,2},{1,3},{2,0},{3,1},{4,6},{5,7},{6,4},{7,5},{8,10},{9,11},{10,... | collective-permute-start | bytes 147464 | tf_op jit(solution)/shard_map/ppermute | solution.py:707
  27.7 1.4 %collective-permute-start.8 = (f32[32,384]{1,0:T(8,128)S(1)}, f32[32,384]{1,0:T(8,128)S(1)}, u32[]{:S(2)}, u32[]{:S(2)}) collective-permute-start(f32[32,384]{1,0:T(8,128)S(1)} %get-tuple-element.38), channel_id=1, source_target_pairs={{0,3},{1,0},{2,1},{3,2},{4,7},{5,4},{6,5},{7,6},{8,11},{9,8},{10,9... | collective-permute-start | bytes 147464 | tf_op jit(solution)/shard_map/ppermute | solution.py:707
  29.1 2.7 %fixed.1 = f32[8,128,128]{2,1,0:T(8,128)S(1)} custom-call(f32[8,128,128]{2,1,0:T(8,128)S(1)} %get-tuple-element.22.rhs, f32[8,128,128]{2,1,0:T(8,128)S(1)} %get-tuple-element.23.pre_ref), custom_call_target="tpu_custom_call" | custom-call | flops 4194304 | bytes 4194304 | tf_op jit(solution)/shard_map/fixed/pallas_call | solution.py:628
  31.8 0.8 %emit.1 = f32[1024,128]{1,0:T(8,128)} custom-call(f32[4608,128]{1,0:T(8,128)S(1)} %get-tuple-element.39.third), custom_call_target="tpu_custom_call" | custom-call | flops 2097152 | bytes 2097152 | tf_op jit(solution)/shard_map/emit/pallas_call | solution.py:628
  32.6 1.6 %post.1 = f32[3,32,1024]{2,1,0:T(8,128)} custom-call(f32[136,128]{1,0:T(8,128)S(1)} %get-tuple-element.21.own_ref, f32[8,128,128]{2,1,0:T(8,128)S(1)} %fixed.1, f32[32,384]{1,0:T(8,128)S(1)} %get-tuple-element.35.rest_0_, f32[32,384]{1,0:T(8,128)S(1)} %collective-permute-done.6.rest_1_, f32[32,384]{1,0:T(8,128)S(1)} %collective-permute-done.7.rest_2_, ...), custom_call_target="tpu_custom_call" | custom-call | tf_op jit(solution)/shard_map/post/pallas_call | solution.py:628
  (4 shorter events, 0.0 us)
Async XLA Ops:
  4.1 5.7 %collective-permute-start.2 = (f32[136,128]{1,0:T(8,128)S(1)}, f32[136,128]{1,0:T(8,128)S(1)}, u32[]{:S(2)}, u32[]{:S(2)}) collective-permute-start(f32[136,128]{1,0:T(8,128)S(1)} %get-tuple-element.26), channel_id=1, source_target_pairs={{0,3},{1,0},{2,1},{3,2},{4,7},{5,4},{6,5},{7,6},{8,11},{9,8},{10,9... | collective-permute-start | bytes 208904 | tf_op jit(solution)/shard_map/ppermute | solution.py:679
  5.1 4.7 %collective-permute-start = (f32[136,128]{1,0:T(8,128)S(1)}, f32[136,128]{1,0:T(8,128)S(1)}, u32[]{:S(2)}, u32[]{:S(2)}) collective-permute-start(f32[136,128]{1,0:T(8,128)S(1)} %get-tuple-element.21.own_ref), channel_id=1, source_target_pairs={{0,1},{1,2},{2,3},{3,0},{4,5},{5,6},{6,7},{7,4},{8,9},{9,10},{10,1... | collective-permute-start | bytes 208904 | tf_op jit(solution)/shard_map/ppermute | solution.py:679
  5.1 4.7 %collective-permute-start.1 = (f32[104,128]{1,0:T(8,128)S(1)}, f32[104,128]{1,0:T(8,128)S(1)}, u32[]{:S(2)}, u32[]{:S(2)}) collective-permute-start(f32[104,128]{1,0:T(8,128)S(1)} %get-tuple-element.25), channel_id=1, source_target_pairs={{0,2},{1,3},{2,0},{3,1},{4,6},{5,7},{6,4},{7,5},{8,10},{9,11},{10,... | collective-permute-start | bytes 159752 | tf_op jit(solution)/shard_map/ppermute | solution.py:679
  12.1 4.2 %collective-permute-start.3 = (f32[104,128]{1,0:T(8,128)S(1)}, f32[104,128]{1,0:T(8,128)S(1)}, u32[]{:S(2)}, u32[]{:S(2)}) collective-permute-start(f32[104,128]{1,0:T(8,128)S(1)} %get-tuple-element.28), channel_id=1, source_target_pairs={{0,4},{4,0},{1,5},{5,1},{2,6},{6,2},{3,7},{7,3},{8,12},{12,8},{9,1... | collective-permute-start | bytes 159752 | tf_op jit(solution)/shard_map/ppermute | solution.py:645
  16.4 8.0 %collective-permute-start.4 = (f32[136,128]{1,0:T(8,128)S(1)}, f32[136,128]{1,0:T(8,128)S(1)}, u32[]{:S(2)}, u32[]{:S(2)}) collective-permute-start(f32[136,128]{1,0:T(8,128)S(1)} %get-tuple-element.33), channel_id=1, source_target_pairs={{0,8},{16,24},{8,0},{24,16},{1,9},{17,25},{9,1},{25,17},{2,10},{18... | collective-permute-start | bytes 208904 | tf_op jit(solution)/shard_map/ppermute | solution.py:645
  16.9 7.5 %collective-permute-start.5 = (f32[136,128]{1,0:T(8,128)S(1)}, f32[136,128]{1,0:T(8,128)S(1)}, u32[]{:S(2)}, u32[]{:S(2)}) collective-permute-start(f32[136,128]{1,0:T(8,128)S(1)} %get-tuple-element.34), channel_id=1, source_target_pairs={{8,16},{16,8},{9,17},{17,9},{10,18},{18,10},{11,19},{19,11},{12,20... | collective-permute-start | bytes 208904 | tf_op jit(solution)/shard_map/ppermute | solution.py:645
  27.2 5.4 %collective-permute-start.6 = (f32[32,384]{1,0:T(8,128)S(1)}, f32[32,384]{1,0:T(8,128)S(1)}, u32[]{:S(2)}, u32[]{:S(2)}) collective-permute-start(f32[32,384]{1,0:T(8,128)S(1)} %get-tuple-element.36), channel_id=1, source_target_pairs={{0,1},{1,2},{2,3},{3,0},{4,5},{5,6},{6,7},{7,4},{8,9},{9,10},{10,1... | collective-permute-start | bytes 147464 | tf_op jit(solution)/shard_map/ppermute | solution.py:707
  27.3 5.4 %collective-permute-start.7 = (f32[32,384]{1,0:T(8,128)S(1)}, f32[32,384]{1,0:T(8,128)S(1)}, u32[]{:S(2)}, u32[]{:S(2)}) collective-permute-start(f32[32,384]{1,0:T(8,128)S(1)} %get-tuple-element.37), channel_id=1, source_target_pairs={{0,2},{1,3},{2,0},{3,1},{4,6},{5,7},{6,4},{7,5},{8,10},{9,11},{10,... | collective-permute-start | bytes 147464 | tf_op jit(solution)/shard_map/ppermute | solution.py:707
  27.7 5.0 %collective-permute-start.8 = (f32[32,384]{1,0:T(8,128)S(1)}, f32[32,384]{1,0:T(8,128)S(1)}, u32[]{:S(2)}, u32[]{:S(2)}) collective-permute-start(f32[32,384]{1,0:T(8,128)S(1)} %get-tuple-element.38), channel_id=1, source_target_pairs={{0,3},{1,0},{2,1},{3,2},{4,7},{5,4},{6,5},{7,6},{8,11},{9,8},{10,9... | collective-permute-start | bytes 147464 | tf_op jit(solution)/shard_map/ppermute | solution.py:707
where the time goes:
time: 34.9 us; the launch traced here: 34.3 us
  Pallas kernels  17.9 us (51%)
  starting transfers between devices  9.03 us (26%)
  waiting for transfers between devices  5.97 us (17%)
  between operations  1.38 us (4%)
    pallas_call x10, Pallas kernels, call(): pl.pallas_call(kernel, name=name, out_shape=[jax.ShapeDtypeStruct(s, F32)...  17.9 us
    ppermute x3, starting transfers between devices, swap_pairs(): got.append(lax.ppermute(send, axis, pairs + [(b, a) for a, b in pairs]))  5.1 us
    ppermute x3, waiting for transfers between devices, per_device(): msgs = [lax.ppermute(m, 'gz', ring(s)) for s, m in zip(shifts, sends)]  3.01 us
    ppermute x3, waiting for transfers between devices, swap_pairs(): got.append(lax.ppermute(send, axis, pairs + [(b, a) for a, b in pairs]))  2.96 us
    ppermute x3, starting transfers between devices, per_device(): msgs = [lax.ppermute(m, 'gz', ring(s)) for s, m in zip(shifts, sends)]  2.08 us
    ppermute x3, starting transfers between devices, per_device(): back = [cuts[0]] + [lax.ppermute(cuts[s], 'gz', ring(s)) for s in shifts]  1.85 us
  transfers between devices with their start and end apart: 9, of which 2 were waited for; matrix products, arithmetic and copies ran while one was open for 0% of the time, Pallas kernels for 24%

commit v1 on v0

--- a/solution.py
+++ b/solution.py
@@ -6,6 +6,7 @@
 from jax.experimental import pallas as pl
 from jax.experimental.pallas import tpu as pltpu
 from jax.sharding import PartitionSpec as P
+
 
 LANES = 128
 SUB = 8
@@ -86,17 +87,17 @@
                 ref[t, pl.ds(row, SUB), :] = gap
 
 
-def pack_face(ref, plan, low):
-    outs = []
+def pack_faces(ref, plan, starts):
     lane = iota((SUB, LANES), 1)
-    start = 0 if low else plan.cz - RIM
-    for j in range(plan.cy // SUB):
-        acc = jnp.zeros((SUB, LANES), F32)
-        for x in range(plan.cx):
-            v = pltpu.roll(ref[pl.ds(x * plan.cy + j * SUB, SUB), :], (4 * x - start) % LANES, 1)
-            acc = jnp.where(lane // 4 == x, v, acc)
-        outs.append(acc)
-    return outs
+    count = plan.cy // SUB
+    packed = [[jnp.zeros((SUB, LANES), F32)] * count for _ in starts]
+    for x in range(plan.cx):
+        mask = lane // 4 == x
+        for j in range(count):
+            v = ref[pl.ds(x * plan.cy + j * SUB, SUB), :]
+            for face, start in zip(packed, starts):
+                face[j] = jnp.where(mask, pltpu.roll(v, (4 * x - start) % LANES, 1), face[j])
+    return packed
 
 
 def patch_code(plan, count, corner_ref, p):
@@ -108,12 +109,20 @@
 
 
 def pre_kernel(plan, count_ref, corner_hbm, fine_hbm, coarse_hbm, rhs, pre_ref, blk, *rest):
-    msg_refs, (fine_ref, res, corner_ref, sems) = rest[:-4], rest[-4:]
-    pe, foot, tiles = plan.pe, plan.foot, plan.tiles
-    copies = [pltpu.make_async_copy(fine_hbm.at[p], fine_ref.at[p], sems.at[p]) for p in range(plan.slots)]
-    at = plan.slots
-    copies.append(pltpu.make_async_copy(coarse_hbm, blk, sems.at[at]))
-    copies.append(pltpu.make_async_copy(corner_hbm, corner_ref, sems.at[at + 1]))
+    msg_refs, (res, corner_ref, sems) = rest[:-3], rest[-3:]
+    pe, foot, tiles, slots = plan.pe, plan.foot, plan.tiles, plan.slots
+    copies = [
+        pltpu.make_async_copy(
+            fine_hbm.at[p, :, pl.ds(t * LANES, LANES)],
+            rhs.at[t, pl.ds(SUB + p * plan.fpitch, pe), :],
+            sems.at[p * tiles + t],
+        )
+        for p in range(slots)
+        for t in range(tiles)
+    ]
+    at = slots * tiles
+    copies.append(pltpu.make_async_copy(corner_hbm, corner_ref, sems.at[at]))
+    copies.append(pltpu.make_async_copy(coarse_hbm, blk, sems.at[at + 1]))
     for copy in copies:
         copy.start()
     zero_gaps(rhs, plan)
@@ -121,23 +130,26 @@
     source, target = iota((4 * LANES, LANES), 0), iota((4 * LANES, LANES), 1)
     place = (source // LANES) * 32 + (source % LANES) // 64 * 16 + source % 32 // 2
     table = jnp.where(place == target, 0.5, 0.0).astype(BF16)
-    for p in range(plan.slots):
-        copies[p].wait()
+    for p in range(slots):
+        for copy in copies[p * tiles : (p + 1) * tiles]:
+            copy.wait()
         start = SUB + p * plan.fpitch
         for j in range(pe // SUB):
-            for t in range(tiles):
-                rhs[t, pl.ds(start + j * SUB, SUB), :] = fine_ref[
-                    p, pl.ds(j * SUB, SUB), t * LANES : (t + 1) * LANES
-                ]
-        for j in range(pe // SUB):
+            rows = pl.ds(start + j * SUB, SUB)
+            values = []
             for t in range(tiles):
                 mid, total = fine_neighbors(rhs, t, start + j * SUB, tiles)
-                pre_ref[t, pl.ds(start + j * SUB, SUB), :] = 0.165 * mid + 0.0225 * total
+                values.append(0.165 * mid + 0.0225 * total)
+            for t, v in enumerate(values):
+                pre_ref[t, rows, :] = v
         for j in range(pe // SUB):
+            rows = pl.ds(start + j * SUB, SUB)
+            values = []
             for t in range(tiles):
                 mid, total = fine_neighbors(pre_ref, t, start + j * SUB, tiles)
-                rows = pl.ds(start + j * SUB, SUB)
-                res[t, rows, :] = rhs[t, rows, :] - (6.0 * mid - total)
+                values.append(rhs[t, rows, :] - (6.0 * mid - total))
+            for t, v in enumerate(values):
+                res[t, rows, :] = v
         lines = []
         for half in range(2):
             cols = []
@@ -155,19 +167,17 @@
         copy.wait()
     lane = iota((SUB, LANES), 1)
     tags = jnp.zeros((SUB, LANES), F32)
-    for p in range(plan.slots):
+    for p in range(slots):
         code = patch_code(plan, count_ref[0], corner_ref, p)
         tags = jnp.where(lane == p, code.astype(F32), tags)
-    packed = {}
+    high, low = pack_faces(blk, plan, (plan.cz - RIM, 0))
     for shift, ref in enumerate(msg_refs, 1):
         at = plan.avg_rows
         ref[pl.ds(at, SUB), :] = tags
         at += SUB
-        for low, wanted in enumerate(plan.faces(shift)):
+        for face, wanted in zip((high, low), plan.faces(shift)):
             if wanted:
-                if low not in packed:
-                    packed[low] = pack_face(blk, plan, low)
-                for j, v in enumerate(packed[low]):
+                for j, v in enumerate(face):
                     ref[pl.ds(at + j * SUB, SUB), :] = v
                 at += plan.zrows
 
@@ -190,7 +200,7 @@
 
 def place_patch(plan, ref, base, code, comp, block=True, rims=True):
     me = lax.axis_index("gz")
-    x0, y0, home, z0 = decode(plan, code)
+    x0, y0, _, z0 = decode(plan, code)
     dz = z0 - me * plan.cz
 
     inside = (dz >= 0) & (dz < plan.cz)
@@ -207,12 +217,14 @@
         lane = iota((plan.foot, LANES), 1)
         window = (lane >= lane0) & (lane < lane0 + plan.foot)
         first = offset + plan.row(x0, y0)
+        halves = [ref[pl.ds(base + half * plan.foot, plan.foot), :] for half in range(2)]
+        values = []
         for y in range(plan.foot):
             half, k = divmod(y * plan.foot, LANES)
-            v = ref[pl.ds(base + half * plan.foot, plan.foot), :]
-            v = pltpu.roll(v, (lane0 + LANES - k) % LANES, 1)
-            rows = pl.ds(first + y, plan.foot, stride=plan.pitch)
-            comp[rows, :] = jnp.where(window, v, comp[rows, :])
+            v = pltpu.roll(halves[half], (lane0 + LANES - k) % LANES, 1)
+            values.append(jnp.where(window, v, comp[pl.ds(first + y, plan.foot, stride=plan.pitch), :]))
+        for y, v in enumerate(values):
+            comp[pl.ds(first + y, plan.foot, stride=plan.pitch), :] = v
 
 
 def flags(axis, size):
@@ -220,23 +232,30 @@
     return index > 0, index < size - 1
 
 
-def fixed_kernel(plan, rhs, pre_ref, out, work):
-    zero_gaps(work, plan)
-    for source, target in ((pre_ref, work), (work, out)):
-
-        def rows8(i, carry):
-            p, j = i // (plan.pe // SUB), i % (plan.pe // SUB)
-            row = pl.multiple_of(SUB + p * plan.fpitch + j * SUB, SUB)
-            for t in range(plan.tiles):
-                mid, total = fine_neighbors(source, t, row, plan.tiles)
-                rows = pl.ds(row, SUB)
-                target[t, rows, :] = 0.1 * mid + 0.15 * (rhs[t, rows, :] + total)
-            return carry
-
-        lax.fori_loop(0, plan.slots * (plan.pe // SUB), rows8, 0)
-
-
-def base_kernel(plan, blk, own_ref, comp):
+def fixed_step(plan, rhs, source, target):
+    def rows8(i, carry):
+        p, j = i // (plan.pe // SUB), i % (plan.pe // SUB)
+        row = pl.multiple_of(SUB + p * plan.fpitch + j * SUB, SUB)
+        rows = pl.ds(row, SUB)
+        values = []
+        for t in range(plan.tiles):
+            mid, total = fine_neighbors(source, t, row, plan.tiles)
+            values.append(0.1 * mid + 0.15 * (rhs[t, rows, :] + total))
+        for t, v in enumerate(values):
+            target[t, rows, :] = v
+        return carry
+
+    lax.fori_loop(0, plan.slots * (plan.pe // SUB), rows8, 0)
+
+
+def late_step(plan, rhs, source, after, target):
+    del after
+    fixed_step(plan, rhs, source, target)
+
+
+def base_kernel(plan, blk, own_ref, rhs, pre_ref, comp, fixed):
+    zero_gaps(fixed, plan)
+    fixed_step(plan, rhs, pre_ref, fixed)
     cx, cy = plan.cx, plan.cy
     end = SUB + RIM * plan.pitch
     for base in (0, plan.crows):
@@ -246,12 +265,11 @@
             comp[pl.ds(base + plan.row(x, cy), SUB), :] = jnp.zeros((SUB, LANES), F32)
     for x in range(cx):
         comp[pl.ds(plan.row(x, 0), cy), :] = blk[pl.ds(x * cy, cy), :]
-        comp[pl.ds(plan.crows + plan.row(x, 0), cy), :] = jnp.zeros((cy, LANES), F32)
     for p in range(plan.slots):
         place_patch(plan, own_ref, p * 2 * plan.foot, message_code(plan, own_ref, p), comp, rims=False)
 
 
-def compose_kernel(plan, n_y, comp_in, own_ref, *rest):
+def compose_kernel(plan, comp_in, own_ref, *rest):
     msg_refs, (comp, *y_sends) = rest[: plan.nz - 1], rest[plan.nz - 1 :]
     del comp_in
     cx, cy = plan.cx, plan.cy
@@ -274,8 +292,7 @@
             rows = pl.ds(plan.crows + plan.row(x, j * SUB), SUB)
             lo = pltpu.roll(lo_face[j], (plan.cz - RIM - 4 * x) % LANES, 1)
             hi = pltpu.roll(hi_face[j], (-4 * x) % LANES, 1)
-            v = jnp.where(lane < RIM, hi, comp[rows, :])
-            comp[rows, :] = jnp.where(lane >= plan.cz - RIM, lo, v)
+            comp[rows, :] = jnp.where(lane >= plan.cz - RIM, lo, jnp.where(lane < RIM, hi, 0.0))
     for p in range(plan.slots):
         for ref in (own_ref, *msg_refs):
             code = message_code(plan, ref, p)
@@ -314,18 +331,20 @@
         comp[pl.ds(plan.crows + plan.row(0, y + k), plan.cx, stride=plan.pitch), :] = rims
 
 
-def xface_kernel(plan, n_y, n_x, comp_in, second_in, *rest):
+def pack_xface(plan, comp, ref, start):
+    at_high = lax.axis_index("gx") % 2 == start
+    first = pl.multiple_of(plan.row(jnp.where(at_high, plan.cx - RIM, 0), 0) - SUB, SUB)
+    rims = [comp[pl.ds(plan.crows + first + i * SUB, SUB), :] for i in range(plan.xrows // SUB)]
+    ref[pl.ds(0, plan.xrows), :] = comp[pl.ds(first, plan.xrows), :]
+    ref[pl.ds(plan.xrows, SUB), :] = pack_rims(rims)
+
+
+def xface_kernel(plan, n_y, comp_in, second_in, *rest):
     y_refs, (comp, second, *x_sends) = rest[:n_y], rest[n_y:]
     del comp_in, second_in, second
     put_yfaces(plan, y_refs, comp)
-    odd = lax.axis_index("gx") % 2
-    for start, ref in enumerate(x_sends):
-        first = pl.multiple_of(plan.row(jnp.where(odd == start, plan.cx - RIM, 0), 0) - SUB, SUB)
-        ref[pl.ds(0, plan.xrows), :] = comp[pl.ds(first, plan.xrows), :]
-        rims = [
-            comp[pl.ds(plan.crows + first + i * SUB, SUB), :] for i in range(plan.xrows // SUB)
-        ]
-        ref[pl.ds(plan.xrows, SUB), :] = pack_rims(rims)
+    for i, ref in enumerate(x_sends):
+        pack_xface(plan, comp, ref, i)
 
 
 def put_yfaces(plan, y_refs, comp):
@@ -333,25 +352,6 @@
     for i, ref in enumerate(y_refs):
         at_high = (odd == 0) if i == 0 else (odd == 1)
         put_yface(plan, ref, comp, jnp.where(at_high, plan.cy, -RIM))
-
-
-def put_xfaces(plan, x_refs, comp):
-    odd = lax.axis_index("gx") % 2
-    for i, ref in enumerate(x_refs):
-        at_high = (odd == 0) if i == 0 else (odd == 1)
-        first = plan.row(jnp.where(at_high, plan.cx, -RIM), 0) - SUB
-        packed = ref[pl.ds(plan.xrows, SUB), :]
-        row = iota((SUB, LANES), 0)
-        n = plan.xrows // SUB
-        for k in range(n):
-            for tile in range(2):
-                v = ref[pl.ds(k * SUB, SUB), :] if tile == 0 else unpack_rim(packed, k)
-                rows = pl.ds(tile * plan.crows + first + k * SUB, SUB)
-                if k == 0:
-                    v = jnp.where(row >= SUB - RIM, v, comp[rows, :])
-                if k == n - 1:
-                    v = jnp.where(row < RIM, v, comp[rows, :])
-                comp[rows, :] = v
 
 
 class Sweeps:
@@ -381,65 +381,87 @@
             sums[i] += pltpu.roll(jnp.where(lane == 0, mids[1 - i], mids[i]), LANES - 1, 1)
         return mids, sums
 
-    def step2(self, x, j):
-        at = self.at(x, j)
-        mids, sums = self.stencil(self.comp, at)
-        for i in range(2):
-            v = 0.165 * mids[i] + 0.0225 * sums[i]
-            v = v * self.ymask if j == self.main else v
-            self.second[pl.ds(i * self.plan.crows + at, SUB), :] = v * self.zmask if i else v
-
-    def step3(self, x, j):
-        at, crows, lane = self.at(x, j), self.plan.crows, self.lane
-        mids, sums = self.stencil(self.second, at)
-        outs = []
-        for i in range(2):
-            v = 0.1 * mids[i] + 0.15 * (self.comp[pl.ds(i * crows + at, SUB), :] + sums[i])
-            v = v * self.ymask if j == self.main else v
-            outs.append(v * self.zmask if i else v)
-        self.third[pl.ds(at, SUB), :] = outs[0]
-        self.third[pl.ds(crows + at, SUB), :] = jnp.where(lane >= LANES - 2, outs[1], outs[0])
-        self.third[pl.ds(2 * crows + at, SUB), :] = jnp.where(lane < 2, outs[1], outs[0])
-
-    def planes(self, step, first, last, tiles, unroll=2):
-        def body(x, carry):
-            for j in tiles:
-                step(x, j)
+    def step2(self, places):
+        values = []
+        for x, j in places:
+            at = self.at(x, j)
+            mids, sums = self.stencil(self.comp, at)
+            for i in range(2):
+                v = 0.165 * mids[i] + 0.0225 * sums[i]
+                v = v * self.ymask if j == self.main else v
+                values.append((i * self.plan.crows + at, v * self.zmask if i else v))
+        for at, v in values:
+            self.second[pl.ds(at, SUB), :] = v
+
+    def step3(self, places):
+        crows, lane = self.plan.crows, self.lane
+        values = []
+        for x, j in places:
+            at = self.at(x, j)
+            mids, sums = self.stencil(self.second, at)
+            outs = []
+            for i in range(2):
+                v = 0.1 * mids[i] + 0.15 * (self.comp[pl.ds(i * crows + at, SUB), :] + sums[i])
+                v = v * self.ymask if j == self.main else v
+                outs.append(v * self.zmask if i else v)
+            values.append((at, outs[0]))
+            values.append((crows + at, jnp.where(lane >= LANES - 2, outs[1], outs[0])))
+            values.append((2 * crows + at, jnp.where(lane < 2, outs[1], outs[0])))
+        for at, v in values:
+            self.third[pl.ds(at, SUB), :] = v
+
+    def planes(self, step, first, last, tiles, group=2):
+        whole = (last + 1 - first) // group
+
+        def body(i, carry):
+            step([(first + i * group + k, j) for k in range(group) for j in tiles])
             return carry
 
-        lax.fori_loop(first, last + 1, body, 0, unroll=unroll)
-
-
-def inner_kernel(plan, comp, second):
-    s = Sweeps(plan, comp, second)
-    s.planes(s.step2, 1, plan.cx - 2, range(1, s.main - 1), unroll=3)
-
-
-def middle_kernel(plan, comp, second_in, second, third):
-    del second_in
+        lax.fori_loop(0, whole, body, 0)
+        for x in range(first + whole * group, last + 1):
+            step([(x, j) for j in tiles])
+
+
+def inner_kernel(plan, comp, second, third):
     s = Sweeps(plan, comp, second, third)
-    s.step2(0, s.main)
-    s.planes(s.step2, 1, plan.cx - 2, (0, s.main - 1, s.main))
-    s.planes(s.step3, 2, plan.cx - 3, range(s.main + 1))
+    s.planes(s.step2, 1, plan.cx - 2, range(s.main))
+    s.planes(s.step3, 2, plan.cx - 3, range(1, s.main - 1))
+
+
+def middle_kernel(plan, comp, second_in, third_in, second, third):
+    del second_in, third_in
+    s = Sweeps(plan, comp, second, third)
+    for y, rim in ((0, -1), (plan.cy - 1, plan.cy)):
+        for base in (0, plan.crows):
+            rows = pl.ds(base + plan.row(0, y), plan.cx, stride=plan.pitch)
+            rims = pl.ds(base + plan.row(0, rim), plan.cx, stride=plan.pitch)
+            second[rows, :] = second[rows, :] + 0.0225 * comp[rims, :]
+    s.planes(s.step2, 0, plan.cx - 2, (s.main,), group=4)
+    s.planes(s.step3, 2, plan.cx - 3, (0, s.main - 1, s.main))
 
 
 def put_xfaces(plan, x_refs, comp):
     odd = lax.axis_index("gx") % 2
+    has_lo, has_hi = flags("gx", plan.nx)
     for i, ref in enumerate(x_refs):
-        at_high = (odd == 0) if i == 0 else (odd == 1)
+        at_high = odd == i
+        has = (at_high & has_hi) | (jnp.logical_not(at_high) & has_lo)
         first = pl.multiple_of(plan.row(jnp.where(at_high, plan.cx, -RIM), 0) - SUB, SUB)
-        packed = ref[pl.ds(plan.xrows, SUB), :]
+        packed = jnp.where(has, ref[pl.ds(plan.xrows, SUB), :], 0.0)
         row = iota((SUB, LANES), 0)
         n = plan.xrows // SUB
+        values = []
         for k in range(n):
             for tile in range(2):
-                v = ref[pl.ds(k * SUB, SUB), :] if tile == 0 else unpack_rim(packed, k)
+                v = jnp.where(has, ref[pl.ds(k * SUB, SUB), :], 0.0) if tile == 0 else unpack_rim(packed, k)
                 rows = pl.ds(tile * plan.crows + first + k * SUB, SUB)
                 if k == 0:
                     v = jnp.where(row >= SUB - RIM, v, comp[rows, :])
                 if k == n - 1:
                     v = jnp.where(row < RIM, v, comp[rows, :])
-                comp[rows, :] = v
+                values.append((rows, v))
+        for rows, v in values:
+            comp[rows, :] = v
 
 
 def edge_kernel(plan, n_x, comp_in, second_in, third_in, own_ref, *rest):
@@ -451,11 +473,9 @@
     s = Sweeps(plan, comp, second, third)
     x_lo, x_hi = flags("gx", plan.nx)
     every = range(s.main + 1)
-    s.step2(-RIM, s.main)
-    s.step2(cx - 2, s.main)
+    s.step2([(-RIM, s.main), (cx - 2, s.main)])
     for x in (-2, -1, 0, cx - 1, cx, cx + 1):
-        for j in every:
-            s.step2(x, j)
+        s.step2([(x, j) for j in every])
     for has, x in ((x_lo, 1 - RIM), (x_hi, cx)):
 
         @pl.when(jnp.logical_not(has))
@@ -463,11 +483,9 @@
             for base in (0, crows):
                 second[pl.ds(base + plan.row(x, -RIM), 2 * pitch), :] = jnp.zeros((2 * pitch, LANES), F32)
 
-    s.step3(1 - RIM, s.main)
-    s.step3(cx - 3, s.main)
+    s.step3([(1 - RIM, s.main), (cx - 3, s.main)])
     for x in (-1, 0, 1, cx - 2, cx - 1, cx):
-        for j in every:
-            s.step3(x, j)
+        s.step3([(x, j) for j in every])
     for has, x in ((x_lo, -1), (x_hi, cx)):
 
         @pl.when(jnp.logical_not(has))
@@ -580,7 +598,7 @@
     for p in range(slots):
         start = SUB + p * plan.fpitch
         ustart = SUB + p * (foot + SUB)
-        for i, (v, k) in enumerate(((lows, 0), (highs, 1))):
+        for v, k in ((lows, 0), (highs, 1)):
             line = v[p * foot : (p + 1) * foot]
             for parity in range(2):
                 yghost[k, pl.ds(start + parity, foot, stride=2), :] = line
@@ -601,6 +619,7 @@
         alive = codes[p] >= 0
         for j in range(pe // SUB):
             rows = pl.ds(start + j * SUB, SUB)
+            values = []
             for t in range(tiles):
                 mid = first[t, rows, :]
                 side = ghost[t, rows, :]
@@ -612,7 +631,9 @@
                 total += pltpu.roll(jnp.where(lane >= LANES - 32, before, mid), 32, 1)
                 total += pltpu.roll(jnp.where(lane < 32, after, mid), LANES - 32, 1)
                 value = fixed[t, rows, :] + (0.1 * mid + 0.15 * total)
-                out_ref[p, pl.ds(j * SUB, SUB), t * LANES : (t + 1) * LANES] = jnp.where(alive, value, 0.0)
+                values.append(jnp.where(alive, value, 0.0))
+            for t, value in enumerate(values):
+                out_ref[p, pl.ds(j * SUB, SUB), t * LANES : (t + 1) * LANES] = value
         copies[p].start()
     for copy in copies:
         copy.wait()
@@ -623,11 +644,10 @@
 SMEM = pl.BlockSpec(memory_space=pltpu.SMEM)
 
 
-def call(kernel, name, outs, args, scratch=(), aliases=None, smem=0, hbm_in=0, hbm_out=0, sems=0, cost=0):
+def call(kernel, outs, args, scratch=(), aliases=None, smem=0, hbm_in=0, hbm_out=0, sems=0, cost=0):
     spaces = [s if isinstance(s, pl.MemoryRef) else pltpu.VMEM(s, F32) for s in scratch]
     return pl.pallas_call(
         kernel,
-        name=name,
         out_shape=[jax.ShapeDtypeStruct(s, F32) for s in outs],
         in_specs=[SMEM] * smem + [HBM] * hbm_in + [VMEM] * (len(args) - hbm_in - smem),
         out_specs=[HBM] * hbm_out + [VMEM] * (len(outs) - hbm_out),
@@ -638,15 +658,22 @@
     )(*args)
 
 
-def swap_pairs(axis, size, sends):
+def swap_pairs(axis, size, sends, beside=None):
     got = []
     for start, send in enumerate(sends):
         pairs = [(i, i + 1) for i in range(start, size - 1, 2)]
-        got.append(lax.ppermute(send, axis, pairs + [(b, a) for a, b in pairs]))
+        pairs += [(b, a) for a, b in pairs]
+        names = axis
+        if beside and len(pairs) < size:
+            alone = set(range(size)) - {a for a, _ in pairs}
+            names = (axis, "gz")
+            pairs = [(a * beside + g, b * beside + g) for a, b in pairs for g in range(beside)]
+            pairs += [(a * beside + g, a * beside + (g ^ 1)) for a in sorted(alone) for g in range(beside)]
+        got.append(lax.ppermute(send, names, pairs))
     return got
 
 
-def per_device(fine_rhs, coarse_rhs, patch_count, patch_corner):
+def cycle(fine_rhs, coarse_rhs, patch_count, patch_corner):
     plan = Plan(fine_rhs.shape, coarse_rhs.shape)
     fine_shape = (plan.tiles, plan.frows, LANES)
     block_shape = (plan.cx * plan.cy, plan.cz)
@@ -659,56 +686,51 @@
     bind = functools.partial
     rhs, pre, block, *sends = call(
         bind(pre_kernel, plan),
-        "pre",
         [fine_shape, fine_shape, block_shape] + [(plan.msg_rows(s), LANES) for s in shifts],
         [patch_count]
         + [
             pltpu.with_memory_space_constraint(a, pltpu.HBM)
             for a in (patch_corner, fine_rhs, coarse_rhs.reshape(block_shape))
         ],
-        scratch=(fine_rhs.shape, fine_shape, pltpu.VMEM(patch_corner.shape, jnp.int32)),
+        scratch=(fine_shape, pltpu.VMEM(patch_corner.shape, jnp.int32)),
         smem=1,
         hbm_in=3,
-        sems=plan.slots + 2,
+        sems=plan.slots * plan.tiles + 2,
     )
     own = sends[0]
 
     def ring(s):
         return [(i, (i + s) % plan.nz) for i in range(plan.nz)]
 
-    msgs = [lax.ppermute(m, "gz", ring(s)) for s, m in zip(shifts, sends)]
-    (comp,) = call(bind(base_kernel, plan), "base", [comp_shape], (block, own), cost=4 << 20)
-    (fixed,) = call(
-        bind(fixed_kernel, plan), "fixed", [fine_shape], (rhs, pre), scratch=(fine_shape,), cost=4 << 20
-    )
-    comp, *ysends = call(
-        bind(compose_kernel, plan, n_y), "compose", [comp_shape] + [yshape] * n_y, (comp, own, *msgs), aliases={0: 0}
-    )
+    msgs = []
+    for s, m in zip(shifts, sends):
+        msgs.append(lax.ppermute(m, "gz", ring(s)))
+    comp, fixed = call(bind(base_kernel, plan), [comp_shape, fine_shape], (block, own, rhs, pre), cost=4 << 20)
+    comp, *ysends = call(bind(compose_kernel, plan), [comp_shape] + [yshape] * n_y, (comp, own, *msgs), aliases={0: 0})
     ygot = swap_pairs("gy", plan.ny, ysends)
-    (second,) = call(bind(inner_kernel, plan), "inner", [comp_shape], (comp,), cost=4 << 20)
+    second, third = call(bind(inner_kernel, plan), [comp_shape, third_shape], (comp,), cost=4 << 20)
     comp, second, *xsends = call(
-        bind(xface_kernel, plan, n_y, n_x),
-        "xface",
+        bind(xface_kernel, plan, n_y),
         [comp_shape, comp_shape] + [xshape] * n_x,
         (comp, second, *ygot),
         aliases={0: 0, 1: 1},
     )
-    xgot = swap_pairs("gx", plan.nx, xsends)
+    xgot = swap_pairs("gx", plan.nx, xsends, beside=plan.nz if plan.nz % 2 == 0 else None)
     second, third = call(
-        bind(middle_kernel, plan), "middle", [comp_shape, third_shape], (comp, second), aliases={1: 0}, cost=8 << 20
+        bind(middle_kernel, plan), [comp_shape, third_shape], (comp, second, third), aliases={1: 0, 2: 1}, cost=8 << 20
     )
     _, _, third, *cuts = call(
         bind(edge_kernel, plan, n_x),
-        "edge",
         [comp_shape, comp_shape, third_shape] + [eshape] * plan.nz,
         (comp, second, third, own, *xgot, *msgs),
         aliases={0: 0, 1: 1, 2: 2},
     )
     back = [cuts[0]] + [lax.ppermute(cuts[s], "gz", ring(s)) for s in shifts]
-    (out,) = call(bind(emit_kernel, plan), "emit", [block_shape], (third,), cost=2 << 20)
+    (out,) = call(bind(emit_kernel, plan), [block_shape], (third,), cost=2 << 20)
+    tiny = lax.slice_in_dim(cuts[0], 0, SUB, axis=0)
+    (fixed,) = call(bind(late_step, plan), [fine_shape], (rhs, fixed, tiny), cost=4 << 20)
     (fine,) = call(
         bind(post_kernel, plan),
-        "post",
         [fine_rhs.shape],
         (own, fixed, *back),
         scratch=(
@@ -726,7 +748,7 @@
 
 def solution(mesh):
     return jax.shard_map(
-        per_device,
+        cycle,
         mesh=mesh,
         in_specs=(
             P(("gx", "gy", "gz"), None, None),

time: 34.9 us -> 32.4 us (0.928)
  the two profiles are of different devices: /device:TPU:10 before, /device:TPU:0 now
where the time goes in v1:
time: 32.4 us; the launch traced here: 32.2 us
  Pallas kernels  17.2 us (53%)
  starting transfers between devices  11 us (34%)
  waiting for transfers between devices  2.62 us (8%)
  between operations  1.39 us (4%)
    pallas_call x10, Pallas kernels, call(): pl.pallas_call(kernel, out_shape=[jax.ShapeDtypeStruct(s, F32) for s in o...  17.2 us
    ppermute x3, starting transfers between devices, cycle(): back = [cuts[0]] + [lax.ppermute(cuts[s], 'gz', ring(s)) for s in shifts]  4.32 us
    ppermute x3, starting transfers between devices, cycle(): msgs.append(lax.ppermute(m, 'gz', ring(s)))  3.56 us
    ppermute x3, starting transfers between devices, swap_pairs(): got.append(lax.ppermute(send, names, pairs))  3.09 us
    ppermute x3, waiting for transfers between devices, cycle(): msgs.append(lax.ppermute(m, 'gz', ring(s)))  1.94 us
    ppermute x3, waiting for transfers between devices, swap_pairs(): got.append(lax.ppermute(send, names, pairs))  0.68 us
  transfers between devices with their start and end apart: 9, of which 2 were waited for; matrix products, arithmetic and copies ran while one was open for 0% of the time, Pallas kernels for 28%

profile of v1, /device:TPU:0, one launch (start us, length us, event | category | flops | bytes accessed | tf_op | source)
XLA Modules:
  0.0 32.2 jit_solution(7832185763089425708)
XLA Ops:
  1.3 3.0 %shard_map.59 = (f32[8,128,128]{2,1,0:T(8,128)S(1)}, f32[8,128,128]{2,1,0:T(8,128)S(1)}, f32[1024,128]{1,0:T(8,128)S(1)}, f32[136,128]{1,0:T(8,128)S(1)}, f32[10...) custom-call(s32[1]{0:T(128)S(6)} %copy.22.count_ref, s32[3,3]{1,0:T(4,128)} %corner_hbm.1, f32[3,32,1024]{2,1,0:T(8,128)} %fine_hbm.1, ...), custom_call_target="tpu_custom_call" | custom-call | tf_op jit(solution)/shard_map/pallas_call | solution.py:649
  4.2 2.5 %collective-permute-start.2 = (f32[136,128]{1,0:T(8,128)S(1)}, f32[136,128]{1,0:T(8,128)S(1)}, u32[]{:S(2)}, u32[]{:S(2)}) collective-permute-start(f32[136,128]{1,0:T(8,128)S(1)} %get-tuple-element.32), channel_id=1, source_target_pairs={{0,3},{1,0},{2,1},{3,2},{4,7},{5,4},{6,5},{7,6},{8,11},{9,8},{10,9... | collective-permute-start | bytes 208904 | tf_op jit(solution)/shard_map/ppermute | solution.py:707
  6.7 1.1 %collective-permute-start.1 = (f32[104,128]{1,0:T(8,128)S(1)}, f32[104,128]{1,0:T(8,128)S(1)}, u32[]{:S(2)}, u32[]{:S(2)}) collective-permute-start(f32[104,128]{1,0:T(8,128)S(1)} %get-tuple-element.31), channel_id=1, source_target_pairs={{0,2},{1,3},{2,0},{3,1},{4,6},{5,7},{6,4},{7,5},{8,10},{9,11},{10,... | collective-permute-start | bytes 159752 | tf_op jit(solution)/shard_map/ppermute | solution.py:707
  7.8 1.7 %shard_map.60 = (f32[3072,128]{1,0:T(8,128)S(1)}, f32[8,128,128]{2,1,0:T(8,128)S(1)}) custom-call(f32[1024,128]{1,0:T(8,128)S(1)} %get-tuple-element.27.blk, f32[136,128]{1,0:T(8,128)S(1)} %get-tuple-element.25.own_ref, f32[8,128,128]{2,1,0:T(8,128)S(1)} %get-tuple-element.26.rhs, f32[8,128,128]{2,1,0:T(8,128)S(1)} %get-tuple-element.28.pre_ref), custom_call_target="tpu_custom_call" | custom-call | flops 4194304 | bytes 4194304 | tf_op jit(solution)/shard_map/pallas_call | solution.py:649
  9.5 1.9 %collective-permute-done.1.rest_1_.rest_3_ = f32[104,128]{1,0:T(8,128)S(1)} collective-permute-done((f32[104,128]{1,0:T(8,128)S(1)}, f32[104,128]{1,0:T(8,128)S(1)}, u32[]{:S(2)}, u32[]{:S(2)}) %collective-permute-start.1) | collective-permute-done | bytes 53280 | tf_op jit(solution)/shard_map/ppermute | solution.py:707
  11.4 0.0 collective-permute-done.2.rest_2_.rest_4_
  11.4 0.0 collective-permute-done.rest_0_.rest_2_
  11.4 1.7 %shard_map.61 = (f32[3072,128]{1,0:T(8,128)S(1)}, f32[104,128]{1,0:T(8,128)S(1)}) custom-call(f32[3072,128]{1,0:T(8,128)S(1)} %get-tuple-element.30.comp_in, f32[136,128]{1,0:T(8,128)S(1)} %get-tuple-element.25.own_ref, f32[136,128]{1,0:T(8,128)S(1)} %collective-permute-done.rest_0_.rest_2_, ...), custom_call_target="tpu_custom_call", output_to_operand_aliasing={{0}: (0, {})} | custom-call | tf_op jit(solution)/shard_map/pallas_call | solution.py:649
  13.1 1.6 %collective-permute-start.3 = (f32[104,128]{1,0:T(8,128)S(1)}, f32[104,128]{1,0:T(8,128)S(1)}, u32[]{:S(2)}, u32[]{:S(2)}) collective-permute-start(f32[104,128]{1,0:T(8,128)S(1)} %get-tuple-element.35), channel_id=1, source_target_pairs={{0,4},{4,0},{1,5},{5,1},{2,6},{6,2},{3,7},{7,3},{8,12},{12,8},{9,1... | collective-permute-start | bytes 159752 | tf_op jit(solution)/shard_map/ppermute | solution.py:672
  14.7 2.9 %shard_map.62 = (f32[3072,128]{1,0:T(8,128)S(1)}, f32[4608,128]{1,0:T(8,128)S(1)}) custom-call(f32[3072,128]{1,0:T(8,128)S(1)} %get-tuple-element.33.comp.comp_in), custom_call_target="tpu_custom_call" | custom-call | flops 4194304 | bytes 4194304 | tf_op jit(solution)/shard_map/pallas_call | solution.py:649
  17.6 0.2 shard_map.63
  17.7 1.5 %collective-permute-start.4 = (f32[136,128]{1,0:T(8,128)S(1)}, f32[136,128]{1,0:T(8,128)S(1)}, u32[]{:S(2)}, u32[]{:S(2)}) collective-permute-start(f32[136,128]{1,0:T(8,128)S(1)} %get-tuple-element.41), channel_id=1, source_target_pairs={{0,8},{16,24},{8,0},{24,16},{1,9},{17,25},{9,1},{25,17},{2,10},{18... | collective-permute-start | bytes 208904 | tf_op jit(solution)/shard_map/ppermute | solution.py:672
  19.3 0.0 collective-permute-start.5
  19.3 2.2 %shard_map.64 = (f32[3072,128]{1,0:T(8,128)S(1)}, f32[4608,128]{1,0:T(8,128)S(1)}) custom-call(f32[3072,128]{1,0:T(8,128)S(1)} %get-tuple-element.36.comp.comp_in, f32[3072,128]{1,0:T(8,128)S(1)} %get-tuple-element.37.second_in, f32[4608,128]{1,0:T(8,128)S(1)} %get-tuple-element.38.third_in), custom_call_target="tpu_custom_call", output_to_operand_aliasing={{0}: (1, {}), {1}: (2, {})} | custom-call | flops 8388608 | bytes 8388608 | tf_op jit(solution)/shard_map/pallas_call | solution.py:649
  21.4 0.7 %collective-permute-done.4.rest_0_ = f32[136,128]{1,0:T(8,128)S(1)} collective-permute-done((f32[136,128]{1,0:T(8,128)S(1)}, f32[136,128]{1,0:T(8,128)S(1)}, u32[]{:S(2)}, u32[]{:S(2)}) %collective-permute-start.4) | collective-permute-done | bytes 69664 | tf_op jit(solution)/shard_map/ppermute | solution.py:672
  22.1 0.0 collective-permute-done.5.rest_1_
  22.1 1.9 %shard_map.65 = (f32[3072,128]{1,0:T(8,128)S(1)}, f32[3072,128]{1,0:T(8,128)S(1)}, f32[4608,128]{1,0:T(8,128)S(1)}, f32[32,384]{1,0:T(8,128)S(1)}, f32[32,384]{1...) custom-call(f32[3072,128]{1,0:T(8,128)S(1)} %get-tuple-element.36.co, ...), custom_call_target="tpu_custom_call", output_to_operand_aliasing={{0}: (0, {}), {1}: (1, {}), {2}: (2, {})} | custom-call | tf_op jit(solution)/shard_map/pallas_call | solution.py:649
  24.0 0.1 collective-permute-start.6
  24.1 2.9 %collective-permute-start.7 = (f32[32,384]{1,0:T(8,128)S(1)}, f32[32,384]{1,0:T(8,128)S(1)}, u32[]{:S(2)}, u32[]{:S(2)}) collective-permute-start(f32[32,384]{1,0:T(8,128)S(1)} %get-tuple-element.45), channel_id=1, source_target_pairs={{0,2},{1,3},{2,0},{3,1},{4,6},{5,7},{6,4},{7,5},{8,10},{9,11},{10,... | collective-permute-start | bytes 147464 | tf_op jit(solution)/shard_map/ppermute | solution.py:728
  27.0 1.4 %collective-permute-start.8 = (f32[32,384]{1,0:T(8,128)S(1)}, f32[32,384]{1,0:T(8,128)S(1)}, u32[]{:S(2)}, u32[]{:S(2)}) collective-permute-start(f32[32,384]{1,0:T(8,128)S(1)} %get-tuple-element.46), channel_id=1, source_target_pairs={{0,3},{1,0},{2,1},{3,2},{4,7},{5,4},{6,5},{7,6},{8,11},{9,8},{10,9... | collective-permute-start | bytes 147464 | tf_op jit(solution)/shard_map/ppermute | solution.py:728
  28.3 0.8 %shard_map.68 = f32[1024,128]{1,0:T(8,128)} custom-call(f32[4608,128]{1,0:T(8,128)S(1)} %get-tuple-element.47.third), custom_call_target="tpu_custom_call" | custom-call | flops 2097152 | bytes 2097152 | tf_op jit(solution)/shard_map/pallas_call | solution.py:649
  29.2 1.4 %shard_map.66.fixed = f32[8,128,128]{2,1,0:T(8,128)S(1)} custom-call(f32[8,128,128]{2,1,0:T(8,128)S(1)} %get-tuple-element.26.rhs, f32[8,128,128]{2,1,0:T(8,128)S(1)} %get-tuple-element.29.source, f32[8,384]{1,0:T(8,128)S(1)} %slice.3.after), custom_call_target="tpu_custom_call" | custom-call | flops 4194304 | bytes 4194304 | tf_op jit(solution)/shard_map/pallas_call | solution.py:649
  30.5 0.0 collective-permute-done.6.rest_1_
  30.6 1.6 %shard_map.67 = f32[3,32,1024]{2,1,0:T(8,128)} custom-call(f32[136,128]{1,0:T(8,128)S(1)} %get-tuple-element.25.own_ref, f32[8,128,128]{2,1,0:T(8,128)S(1)} %shard_map.66.fixed, f32[32,384]{1,0:T(8,128)S(1)} %get-tuple-element.43.rest_0_, f32[32,384]{1,0:T(8,128)S(1)} %collective-permute-done.6.rest_1_, f32[32,384]{1,0:T(8,128)S(1)} %collective-permute-done.7.rest_2_, ...), custom_call_target="tpu_custom_call" | custom-call | tf_op jit(solution)/shard_map/pallas_call | solution.py:649
  (5 shorter events, 0.0 us)
Async XLA Ops:
  4.2 7.2 %collective-permute-start.2 = (f32[136,128]{1,0:T(8,128)S(1)}, f32[136,128]{1,0:T(8,128)S(1)}, u32[]{:S(2)}, u32[]{:S(2)}) collective-permute-start(f32[136,128]{1,0:T(8,128)S(1)} %get-tuple-element.32), channel_id=1, source_target_pairs={{0,3},{1,0},{2,1},{3,2},{4,7},{5,4},{6,5},{7,6},{8,11},{9,8},{10,9... | collective-permute-start | bytes 208904 | tf_op jit(solution)/shard_map/ppermute | solution.py:707
  6.7 4.7 %collective-permute-start = (f32[136,128]{1,0:T(8,128)S(1)}, f32[136,128]{1,0:T(8,128)S(1)}, u32[]{:S(2)}, u32[]{:S(2)}) collective-permute-start(f32[136,128]{1,0:T(8,128)S(1)} %get-tuple-element.25.own_ref), channel_id=1, source_target_pairs={{0,1},{1,2},{2,3},{3,0},{4,5},{5,6},{6,7},{7,4},{8,9},{9,10},{10,1... | collective-permute-start | bytes 208904 | tf_op jit(solution)/shard_map/ppermute | solution.py:707
  6.7 4.7 %collective-permute-start.1 = (f32[104,128]{1,0:T(8,128)S(1)}, f32[104,128]{1,0:T(8,128)S(1)}, u32[]{:S(2)}, u32[]{:S(2)}) collective-permute-start(f32[104,128]{1,0:T(8,128)S(1)} %get-tuple-element.31), channel_id=1, source_target_pairs={{0,2},{1,3},{2,0},{3,1},{4,6},{5,7},{6,4},{7,5},{8,10},{9,11},{10,... | collective-permute-start | bytes 159752 | tf_op jit(solution)/shard_map/ppermute | solution.py:707
  13.1 4.4 %collective-permute-start.3 = (f32[104,128]{1,0:T(8,128)S(1)}, f32[104,128]{1,0:T(8,128)S(1)}, u32[]{:S(2)}, u32[]{:S(2)}) collective-permute-start(f32[104,128]{1,0:T(8,128)S(1)} %get-tuple-element.35), channel_id=1, source_target_pairs={{0,4},{4,0},{1,5},{5,1},{2,6},{6,2},{3,7},{7,3},{8,12},{12,8},{9,1... | collective-permute-start | bytes 159752 | tf_op jit(solution)/shard_map/ppermute | solution.py:672
  17.7 4.4 %collective-permute-start.4 = (f32[136,128]{1,0:T(8,128)S(1)}, f32[136,128]{1,0:T(8,128)S(1)}, u32[]{:S(2)}, u32[]{:S(2)}) collective-permute-start(f32[136,128]{1,0:T(8,128)S(1)} %get-tuple-element.41), channel_id=1, source_target_pairs={{0,8},{16,24},{8,0},{24,16},{1,9},{17,25},{9,1},{25,17},{2,10},{18... | collective-permute-start | bytes 208904 | tf_op jit(solution)/shard_map/ppermute | solution.py:672
  19.3 2.8 %collective-permute-start.5 = (f32[136,128]{1,0:T(8,128)S(1)}, f32[136,128]{1,0:T(8,128)S(1)}, u32[]{:S(2)}, u32[]{:S(2)}) collective-permute-start(f32[136,128]{1,0:T(8,128)S(1)} %get-tuple-element.42), channel_id=1, source_target_pairs={{8,16},{9,17},{10,18},{11,19},{16,8},{17,9},{18,10},{19,11},{0,1},... | collective-permute-start | bytes 208904 | tf_op jit(solution)/shard_map/ppermute | solution.py:672
  24.0 6.5 %collective-permute-start.6 = (f32[32,384]{1,0:T(8,128)S(1)}, f32[32,384]{1,0:T(8,128)S(1)}, u32[]{:S(2)}, u32[]{:S(2)}) collective-permute-start(f32[32,384]{1,0:T(8,128)S(1)} %get-tuple-element.44), channel_id=1, source_target_pairs={{0,1},{1,2},{2,3},{3,0},{4,5},{5,6},{6,7},{7,4},{8,9},{9,10},{10,1... | collective-permute-start | bytes 147464 | tf_op jit(solution)/shard_map/ppermute | solution.py:728
  24.1 6.5 %collective-permute-start.7 = (f32[32,384]{1,0:T(8,128)S(1)}, f32[32,384]{1,0:T(8,128)S(1)}, u32[]{:S(2)}, u32[]{:S(2)}) collective-permute-start(f32[32,384]{1,0:T(8,128)S(1)} %get-tuple-element.45), channel_id=1, source_target_pairs={{0,2},{1,3},{2,0},{3,1},{4,6},{5,7},{6,4},{7,5},{8,10},{9,11},{10,... | collective-permute-start | bytes 147464 | tf_op jit(solution)/shard_map/ppermute | solution.py:728
  27.0 3.6 %collective-permute-start.8 = (f32[32,384]{1,0:T(8,128)S(1)}, f32[32,384]{1,0:T(8,128)S(1)}, u32[]{:S(2)}, u32[]{:S(2)}) collective-permute-start(f32[32,384]{1,0:T(8,128)S(1)} %get-tuple-element.46), channel_id=1, source_target_pairs={{0,3},{1,0},{2,1},{3,2},{4,7},{5,4},{6,5},{7,6},{8,11},{9,8},{10,9... | collective-permute-start | bytes 147464 | tf_op jit(solution)/shard_map/ppermute | solution.py:728

commit v2 on v1

--- a/solution.py
+++ b/solution.py
@@ -87,17 +87,17 @@
                 ref[t, pl.ds(row, SUB), :] = gap
 
 
-def pack_faces(ref, plan, starts):
+def pack_faces(ref, plan):
     lane = iota((SUB, LANES), 1)
     count = plan.cy // SUB
-    packed = [[jnp.zeros((SUB, LANES), F32)] * count for _ in starts]
+    high, low = [jnp.zeros((SUB, LANES), F32)] * count, [jnp.zeros((SUB, LANES), F32)] * count
     for x in range(plan.cx):
-        mask = lane // 4 == x
+        low_mask, high_mask = lane // 4 == x, (lane + RIM) % LANES // 4 == x
         for j in range(count):
-            v = ref[pl.ds(x * plan.cy + j * SUB, SUB), :]
-            for face, start in zip(packed, starts):
-                face[j] = jnp.where(mask, pltpu.roll(v, (4 * x - start) % LANES, 1), face[j])
-    return packed
+            v = pltpu.roll(ref[pl.ds(x * plan.cy + j * SUB, SUB), :], 4 * x, 1)
+            low[j] = jnp.where(low_mask, v, low[j])
+            high[j] = jnp.where(high_mask, v, high[j])
+    return high, low
 
 
 def patch_code(plan, count, corner_ref, p):
@@ -170,7 +170,7 @@
     for p in range(slots):
         code = patch_code(plan, count_ref[0], corner_ref, p)
         tags = jnp.where(lane == p, code.astype(F32), tags)
-    high, low = pack_faces(blk, plan, (plan.cz - RIM, 0))
+    high, low = pack_faces(blk, plan)
     for shift, ref in enumerate(msg_refs, 1):
         at = plan.avg_rows
         ref[pl.ds(at, SUB), :] = tags
@@ -182,16 +182,17 @@
                 at += plan.zrows
 
 
+def below(value, count):
+    bits = count.bit_length() - 1
+    assert count == 1 << bits
+    return lax.shift_right_arithmetic(value, bits), lax.bitwise_and(value, count - 1)
+
+
 def decode(plan, code):
-    total_z = plan.spots_z * plan.nz
-    spot_z = code % total_z
-    spot = code // total_z
-    return (
-        spot // plan.spots_y * plan.foot,
-        spot % plan.spots_y * plan.foot,
-        spot_z // plan.spots_z,
-        spot_z * plan.foot,
-    )
+    spot, spot_z = below(code, plan.spots_z * plan.nz)
+    spot_x, spot_y = below(spot, plan.spots_y)
+    home, _ = below(spot_z, plan.spots_z)
+    return spot_x * plan.foot, spot_y * plan.foot, home, spot_z * plan.foot
 
 
 def message_code(plan, ref, p):
@@ -213,7 +214,7 @@
     @pl.when(wanted)
     def _():
         offset = jnp.where(inside, 0, plan.crows)
-        lane0 = (dz + plan.cz) % plan.cz
+        lane0 = lax.bitwise_and(dz, plan.cz - 1)
         lane = iota((plan.foot, LANES), 1)
         window = (lane >= lane0) & (lane < lane0 + plan.foot)
         first = offset + plan.row(x0, y0)
@@ -221,7 +222,7 @@
         values = []
         for y in range(plan.foot):
             half, k = divmod(y * plan.foot, LANES)
-            v = pltpu.roll(halves[half], (lane0 + LANES - k) % LANES, 1)
+            v = pltpu.roll(halves[half], lax.bitwise_and(lane0 + LANES - k, LANES - 1), 1)
             values.append(jnp.where(window, v, comp[pl.ds(first + y, plan.foot, stride=plan.pitch), :]))
         for y, v in enumerate(values):
             comp[pl.ds(first + y, plan.foot, stride=plan.pitch), :] = v
@@ -254,6 +255,7 @@
 
 
 def base_kernel(plan, blk, own_ref, rhs, pre_ref, comp, fixed):
+    codes = [message_code(plan, own_ref, p) for p in range(plan.slots)]
     zero_gaps(fixed, plan)
     fixed_step(plan, rhs, pre_ref, fixed)
     cx, cy = plan.cx, plan.cy
@@ -265,13 +267,14 @@
             comp[pl.ds(base + plan.row(x, cy), SUB), :] = jnp.zeros((SUB, LANES), F32)
     for x in range(cx):
         comp[pl.ds(plan.row(x, 0), cy), :] = blk[pl.ds(x * cy, cy), :]
-    for p in range(plan.slots):
-        place_patch(plan, own_ref, p * 2 * plan.foot, message_code(plan, own_ref, p), comp, rims=False)
+    for p, code in enumerate(codes):
+        place_patch(plan, own_ref, p * 2 * plan.foot, code, comp, rims=False)
 
 
 def compose_kernel(plan, comp_in, own_ref, *rest):
     msg_refs, (comp, *y_sends) = rest[: plan.nz - 1], rest[plan.nz - 1 :]
     del comp_in
+    codes = [[message_code(plan, ref, p) for ref in (own_ref, *msg_refs)] for p in range(plan.slots)]
     cx, cy = plan.cx, plan.cy
     lane = iota((SUB, LANES), 1)
     zero = jnp.zeros((SUB, LANES), F32)
@@ -290,12 +293,11 @@
     for x in range(cx):
         for j in range(cy // SUB):
             rows = pl.ds(plan.crows + plan.row(x, j * SUB), SUB)
-            lo = pltpu.roll(lo_face[j], (plan.cz - RIM - 4 * x) % LANES, 1)
+            lo = pltpu.roll(lo_face[j], (-4 * x) % LANES, 1)
             hi = pltpu.roll(hi_face[j], (-4 * x) % LANES, 1)
             comp[rows, :] = jnp.where(lane >= plan.cz - RIM, lo, jnp.where(lane < RIM, hi, 0.0))
     for p in range(plan.slots):
-        for ref in (own_ref, *msg_refs):
-            code = message_code(plan, ref, p)
+        for ref, code in zip((own_ref, *msg_refs), codes[p]):
             place_patch(plan, ref, p * 2 * plan.foot, code, comp, block=ref is not own_ref)
     odd = lax.axis_index("gy") % 2
     for start, ref in enumerate(y_sends):
@@ -468,32 +470,8 @@
     x_refs, msg_refs = rest[:n_x], rest[n_x : n_x + plan.nz - 1]
     comp, second, third, *e_refs = rest[n_x + plan.nz - 1 :]
     del comp_in, second_in, third_in
-    cx, pitch, crows = plan.cx, plan.pitch, plan.crows
-    put_xfaces(plan, x_refs, comp)
-    s = Sweeps(plan, comp, second, third)
-    x_lo, x_hi = flags("gx", plan.nx)
-    every = range(s.main + 1)
-    s.step2([(-RIM, s.main), (cx - 2, s.main)])
-    for x in (-2, -1, 0, cx - 1, cx, cx + 1):
-        s.step2([(x, j) for j in every])
-    for has, x in ((x_lo, 1 - RIM), (x_hi, cx)):
-
-        @pl.when(jnp.logical_not(has))
-        def _():
-            for base in (0, crows):
-                second[pl.ds(base + plan.row(x, -RIM), 2 * pitch), :] = jnp.zeros((2 * pitch, LANES), F32)
-
-    s.step3([(1 - RIM, s.main), (cx - 3, s.main)])
-    for x in (-1, 0, 1, cx - 2, cx - 1, cx):
-        s.step3([(x, j) for j in every])
-    for has, x in ((x_lo, -1), (x_hi, cx)):
-
-        @pl.when(jnp.logical_not(has))
-        def _():
-            for base in (0, crows, 2 * crows):
-                third[pl.ds(base + plan.row(x, -RIM), pitch), :] = jnp.zeros((pitch, LANES), F32)
-
     me = lax.axis_index("gz")
+    cuts = []
     for shift in range(plan.nz):
         tags = msg_refs[plan.nz - shift - 1] if shift else own_ref
         used = 0
@@ -501,14 +479,41 @@
             code = message_code(plan, tags, p)
             x0, y0, home, z0 = decode(plan, code)
             here = (code >= 0) & (home == me)
-
-            @pl.when(here)
-            def _():
-                cut_patch(
-                    plan, third, e_refs[shift], jnp.minimum(used, CAP - 1) * plan.foot, x0, y0, z0 % plan.cz
-                )
-
+            base = jnp.minimum(used, CAP - 1) * plan.foot
+            cuts.append((here, e_refs[shift], base, x0, y0, lax.bitwise_and(z0, plan.cz - 1)))
             used = used + here.astype(jnp.int32)
+    cx, pitch, crows = plan.cx, plan.pitch, plan.crows
+    put_xfaces(plan, x_refs, comp)
+    s = Sweeps(plan, comp, second, third)
+    x_lo, x_hi = flags("gx", plan.nx)
+    every = range(s.main + 1)
+    s.step2([(-2, j) for j in range(s.main + 1)] + [(cx - 2, s.main)])
+    s.step2([(x, j) for x in (-1, 0) for j in every])
+    s.step2([(x, j) for x in (cx - 1, cx) for j in every])
+    s.step2([(cx + 1, j) for j in range(s.main)])
+    for has, x in ((x_lo, 1 - RIM), (x_hi, cx)):
+
+        @pl.when(jnp.logical_not(has))
+        def _():
+            for base in (0, crows):
+                second[pl.ds(base + plan.row(x, -RIM), 2 * pitch), :] = jnp.zeros((2 * pitch, LANES), F32)
+
+    s.step3([(-1, j) for j in every] + [(cx - 3, s.main)])
+    s.step3([(x, j) for x in (0, 1) for j in every])
+    s.step3([(x, j) for x in (cx - 2, cx - 1) for j in every])
+    s.step3([(cx, j) for j in range(s.main)])
+    for has, x in ((x_lo, -1), (x_hi, cx)):
+
+        @pl.when(jnp.logical_not(has))
+        def _():
+            for base in (0, crows, 2 * crows):
+                third[pl.ds(base + plan.row(x, -RIM), pitch), :] = jnp.zeros((pitch, LANES), F32)
+
+    for here, out, base, x0, y0, z0 in cuts:
+
+        @pl.when(here)
+        def _():
+            cut_patch(plan, third, out, base, x0, y0, z0)
 
 
 def cut_patch(plan, third, out, base, x0, y0, z0):
@@ -520,7 +525,7 @@
 
     def put(v, source, target, width):
         tile, k = divmod(target, LANES)
-        v = pltpu.roll(v, (k - source + 2 * LANES) % LANES, 1)
+        v = pltpu.roll(v, lax.bitwise_and(k - source + 2 * LANES, LANES - 1), 1)
         outs[tile] = jnp.where((lane >= k) & (lane < k + width), v, outs[tile])
         if k + width > LANES:
             outs[tile + 1] = jnp.where(lane < k + width - LANES, v, outs[tile + 1])

time: 32.4 us -> 29.9 us (0.923)
  Pallas kernels: 17.2 us -> 14.7 us
    pallas_call x10, Pallas kernels: 17.2 us -> 14.7 us  [call(): pl.pallas_call(kernel, out_shape=[jax.ShapeDtypeStruct(s, F32) for s in o...]
  transfers between devices with their start and end apart: 9 -> 9, of which waited for: 2 -> 2; matrix products, arithmetic and copies ran while one was open for 0% -> 0% of each run, Pallas kernels for 28% -> 29%
where the time goes in v2:
time: 29.9 us; the launch traced here: 29.7 us
  Pallas kernels  14.7 us (49%)
  starting transfers between devices  10.8 us (36%)
  waiting for transfers between devices  2.79 us (9%)
  between operations  1.39 us (5%)
    pallas_call x10, Pallas kernels, call(): pl.pallas_call(kernel, out_shape=[jax.ShapeDtypeStruct(s, F32) for s in o...  14.7 us
    ppermute x3, starting transfers between devices, cycle(): back = [cuts[0]] + [lax.ppermute(cuts[s], 'gz', ring(s)) for s in shifts]  4.18 us
    ppermute x3, starting transfers between devices, cycle(): msgs.append(lax.ppermute(m, 'gz', ring(s)))  3.56 us
    ppermute x3, starting transfers between devices, swap_pairs(): got.append(lax.ppermute(send, names, pairs))  3.11 us
    ppermute x3, waiting for transfers between devices, cycle(): msgs.append(lax.ppermute(m, 'gz', ring(s)))  2.12 us
    ppermute x3, waiting for transfers between devices, swap_pairs(): got.append(lax.ppermute(send, names, pairs))  0.66 us
  transfers between devices with their start and end apart: 9, of which 2 were waited for; matrix products, arithmetic and copies ran while one was open for 0% of the time, Pallas kernels for 29%

profile of v2, /device:TPU:0, one launch (start us, length us, event | category | flops | bytes accessed | tf_op | source)
XLA Modules:
  0.0 29.7 jit_solution(8736009842272639740)
XLA Ops:
  1.3 2.8 %shard_map.59 = (f32[8,128,128]{2,1,0:T(8,128)S(1)}, f32[8,128,128]{2,1,0:T(8,128)S(1)}, f32[1024,128]{1,0:T(8,128)S(1)}, f32[136,128]{1,0:T(8,128)S(1)}, f32[10...) custom-call(s32[1]{0:T(128)S(6)} %copy.22.count_ref, s32[3,3]{1,0:T(4,128)} %corner_hbm.1, f32[3,32,1024]{2,1,0:T(8,128)} %fine_hbm.1, ...), custom_call_target="tpu_custom_call" | custom-call | tf_op jit(solution)/shard_map/pallas_call | solution.py:654
  4.1 2.5 %collective-permute-start.2 = (f32[136,128]{1,0:T(8,128)S(1)}, f32[136,128]{1,0:T(8,128)S(1)}, u32[]{:S(2)}, u32[]{:S(2)}) collective-permute-start(f32[136,128]{1,0:T(8,128)S(1)} %get-tuple-element.32), channel_id=1, source_target_pairs={{0,3},{1,0},{2,1},{3,2},{4,7},{5,4},{6,5},{7,6},{8,11},{9,8},{10,9... | collective-permute-start | bytes 208904 | tf_op jit(solution)/shard_map/ppermute | solution.py:712
  6.6 0.0 collective-permute-start
  6.6 1.1 %collective-permute-start.1 = (f32[104,128]{1,0:T(8,128)S(1)}, f32[104,128]{1,0:T(8,128)S(1)}, u32[]{:S(2)}, u32[]{:S(2)}) collective-permute-start(f32[104,128]{1,0:T(8,128)S(1)} %get-tuple-element.31), channel_id=1, source_target_pairs={{0,2},{1,3},{2,0},{3,1},{4,6},{5,7},{6,4},{7,5},{8,10},{9,11},{10,... | collective-permute-start | bytes 159752 | tf_op jit(solution)/shard_map/ppermute | solution.py:712
  7.7 1.5 %shard_map.60 = (f32[3072,128]{1,0:T(8,128)S(1)}, f32[8,128,128]{2,1,0:T(8,128)S(1)}) custom-call(f32[1024,128]{1,0:T(8,128)S(1)} %get-tuple-element.27.blk, f32[136,128]{1,0:T(8,128)S(1)} %get-tuple-element.25.own_ref, f32[8,128,128]{2,1,0:T(8,128)S(1)} %get-tuple-element.26.rhs, f32[8,128,128]{2,1,0:T(8,128)S(1)} %get-tuple-element.28.pre_ref), custom_call_target="tpu_custom_call" | custom-call | flops 4194304 | bytes 4194304 | tf_op jit(solution)/shard_map/pallas_call | solution.py:654
  9.2 2.1 %collective-permute-done.1.rest_1_.rest_3_ = f32[104,128]{1,0:T(8,128)S(1)} collective-permute-done((f32[104,128]{1,0:T(8,128)S(1)}, f32[104,128]{1,0:T(8,128)S(1)}, u32[]{:S(2)}, u32[]{:S(2)}) %collective-permute-start.1) | collective-permute-done | bytes 53280 | tf_op jit(solution)/shard_map/ppermute | solution.py:712
  11.3 0.0 collective-permute-done.rest_0_.rest_2_
  11.3 0.7 %shard_map.61 = (f32[3072,128]{1,0:T(8,128)S(1)}, f32[104,128]{1,0:T(8,128)S(1)}) custom-call(f32[3072,128]{1,0:T(8,128)S(1)} %get-tuple-element.30.comp_in, f32[136,128]{1,0:T(8,128)S(1)} %get-tuple-element.25.own_ref, f32[136,128]{1,0:T(8,128)S(1)} %collective-permute-done.rest_0_.rest_2_, ...), custom_call_target="tpu_custom_call", output_to_operand_aliasing={{0}: (0, {})} | custom-call | tf_op jit(solution)/shard_map/pallas_call | solution.py:654
  12.0 1.6 %collective-permute-start.3 = (f32[104,128]{1,0:T(8,128)S(1)}, f32[104,128]{1,0:T(8,128)S(1)}, u32[]{:S(2)}, u32[]{:S(2)}) collective-permute-start(f32[104,128]{1,0:T(8,128)S(1)} %get-tuple-element.35), channel_id=1, source_target_pairs={{0,4},{4,0},{1,5},{5,1},{2,6},{6,2},{3,7},{7,3},{8,12},{12,8},{9,1... | collective-permute-start | bytes 159752 | tf_op jit(solution)/shard_map/ppermute | solution.py:677
  13.6 2.9 %shard_map.62 = (f32[3072,128]{1,0:T(8,128)S(1)}, f32[4608,128]{1,0:T(8,128)S(1)}) custom-call(f32[3072,128]{1,0:T(8,128)S(1)} %get-tuple-element.33.comp.comp_in), custom_call_target="tpu_custom_call" | custom-call | flops 4194304 | bytes 4194304 | tf_op jit(solution)/shard_map/pallas_call | solution.py:654
  16.4 0.2 shard_map.63
  16.6 1.5 %collective-permute-start.4 = (f32[136,128]{1,0:T(8,128)S(1)}, f32[136,128]{1,0:T(8,128)S(1)}, u32[]{:S(2)}, u32[]{:S(2)}) collective-permute-start(f32[136,128]{1,0:T(8,128)S(1)} %get-tuple-element.41), channel_id=1, source_target_pairs={{0,8},{16,24},{8,0},{24,16},{1,9},{17,25},{9,1},{25,17},{2,10},{18... | collective-permute-start | bytes 208904 | tf_op jit(solution)/shard_map/ppermute | solution.py:677
  18.1 2.2 %shard_map.64 = (f32[3072,128]{1,0:T(8,128)S(1)}, f32[4608,128]{1,0:T(8,128)S(1)}) custom-call(f32[3072,128]{1,0:T(8,128)S(1)} %get-tuple-element.36.comp.comp_in, f32[3072,128]{1,0:T(8,128)S(1)} %get-tuple-element.37.second_in, f32[4608,128]{1,0:T(8,128)S(1)} %get-tuple-element.38.third_in), custom_call_target="tpu_custom_call", output_to_operand_aliasing={{0}: (1, {}), {1}: (2, {})} | custom-call | flops 8388608 | bytes 8388608 | tf_op jit(solution)/shard_map/pallas_call | solution.py:654
  20.3 0.7 %collective-permute-done.4.rest_0_ = f32[136,128]{1,0:T(8,128)S(1)} collective-permute-done((f32[136,128]{1,0:T(8,128)S(1)}, f32[136,128]{1,0:T(8,128)S(1)}, u32[]{:S(2)}, u32[]{:S(2)}) %collective-permute-start.4) | collective-permute-done | bytes 69664 | tf_op jit(solution)/shard_map/ppermute | solution.py:677
  21.0 0.0 collective-permute-done.5.rest_1_
  21.0 0.7 %shard_map.65 = (f32[3072,128]{1,0:T(8,128)S(1)}, f32[3072,128]{1,0:T(8,128)S(1)}, f32[4608,128]{1,0:T(8,128)S(1)}, f32[32,384]{1,0:T(8,128)S(1)}, f32[32,384]{1...) custom-call(f32[3072,128]{1,0:T(8,128)S(1)} %get-tuple-element.36.co, ...), custom_call_target="tpu_custom_call", output_to_operand_aliasing={{0}: (0, {}), {1}: (1, {}), {2}: (2, {})} | custom-call | tf_op jit(solution)/shard_map/pallas_call | solution.py:654
  21.7 0.1 collective-permute-start.6
  21.8 2.7 %collective-permute-start.7 = (f32[32,384]{1,0:T(8,128)S(1)}, f32[32,384]{1,0:T(8,128)S(1)}, u32[]{:S(2)}, u32[]{:S(2)}) collective-permute-start(f32[32,384]{1,0:T(8,128)S(1)} %get-tuple-element.45), channel_id=1, source_target_pairs={{0,2},{1,3},{2,0},{3,1},{4,6},{5,7},{6,4},{7,5},{8,10},{9,11},{10,... | collective-permute-start | bytes 147464 | tf_op jit(solution)/shard_map/ppermute | solution.py:733
  24.5 1.4 %collective-permute-start.8 = (f32[32,384]{1,0:T(8,128)S(1)}, f32[32,384]{1,0:T(8,128)S(1)}, u32[]{:S(2)}, u32[]{:S(2)}) collective-permute-start(f32[32,384]{1,0:T(8,128)S(1)} %get-tuple-element.46), channel_id=1, source_target_pairs={{0,3},{1,0},{2,1},{3,2},{4,7},{5,4},{6,5},{7,6},{8,11},{9,8},{10,9... | collective-permute-start | bytes 147464 | tf_op jit(solution)/shard_map/ppermute | solution.py:733
  25.9 0.8 %shard_map.68 = f32[1024,128]{1,0:T(8,128)} custom-call(f32[4608,128]{1,0:T(8,128)S(1)} %get-tuple-element.47.third), custom_call_target="tpu_custom_call" | custom-call | flops 2097152 | bytes 2097152 | tf_op jit(solution)/shard_map/pallas_call | solution.py:654
  26.7 1.4 %shard_map.66.fixed = f32[8,128,128]{2,1,0:T(8,128)S(1)} custom-call(f32[8,128,128]{2,1,0:T(8,128)S(1)} %get-tuple-element.26.rhs, f32[8,128,128]{2,1,0:T(8,128)S(1)} %get-tuple-element.29.source, f32[8,384]{1,0:T(8,128)S(1)} %slice.3.after), custom_call_target="tpu_custom_call" | custom-call | flops 4194304 | bytes 4194304 | tf_op jit(solution)/shard_map/pallas_call | solution.py:654
  28.1 0.0 collective-permute-done.7.rest_2_
  28.1 0.0 collective-permute-done.8.rest_3_
  28.1 1.6 %shard_map.67 = f32[3,32,1024]{2,1,0:T(8,128)} custom-call(f32[136,128]{1,0:T(8,128)S(1)} %get-tuple-element.25.own_ref, f32[8,128,128]{2,1,0:T(8,128)S(1)} %shard_map.66.fixed, f32[32,384]{1,0:T(8,128)S(1)} %get-tuple-element.43.rest_0_, f32[32,384]{1,0:T(8,128)S(1)} %collective-permute-done.6.rest_1_, f32[32,384]{1,0:T(8,128)S(1)} %collective-permute-done.7.rest_2_, ...), custom_call_target="tpu_custom_call" | custom-call | tf_op jit(solution)/shard_map/pallas_call | solution.py:654
  (5 shorter events, 0.0 us)
Async XLA Ops:
  4.1 7.2 %collective-permute-start.2 = (f32[136,128]{1,0:T(8,128)S(1)}, f32[136,128]{1,0:T(8,128)S(1)}, u32[]{:S(2)}, u32[]{:S(2)}) collective-permute-start(f32[136,128]{1,0:T(8,128)S(1)} %get-tuple-element.32), channel_id=1, source_target_pairs={{0,3},{1,0},{2,1},{3,2},{4,7},{5,4},{6,5},{7,6},{8,11},{9,8},{10,9... | collective-permute-start | bytes 208904 | tf_op jit(solution)/shard_map/ppermute | solution.py:712
  6.6 4.7 %collective-permute-start = (f32[136,128]{1,0:T(8,128)S(1)}, f32[136,128]{1,0:T(8,128)S(1)}, u32[]{:S(2)}, u32[]{:S(2)}) collective-permute-start(f32[136,128]{1,0:T(8,128)S(1)} %get-tuple-element.25.own_ref), channel_id=1, source_target_pairs={{0,1},{1,2},{2,3},{3,0},{4,5},{5,6},{6,7},{7,4},{8,9},{9,10},{10,1... | collective-permute-start | bytes 208904 | tf_op jit(solution)/shard_map/ppermute | solution.py:712
  6.6 4.7 %collective-permute-start.1 = (f32[104,128]{1,0:T(8,128)S(1)}, f32[104,128]{1,0:T(8,128)S(1)}, u32[]{:S(2)}, u32[]{:S(2)}) collective-permute-start(f32[104,128]{1,0:T(8,128)S(1)} %get-tuple-element.31), channel_id=1, source_target_pairs={{0,2},{1,3},{2,0},{3,1},{4,6},{5,7},{6,4},{7,5},{8,10},{9,11},{10,... | collective-permute-start | bytes 159752 | tf_op jit(solution)/shard_map/ppermute | solution.py:712
  12.0 4.4 %collective-permute-start.3 = (f32[104,128]{1,0:T(8,128)S(1)}, f32[104,128]{1,0:T(8,128)S(1)}, u32[]{:S(2)}, u32[]{:S(2)}) collective-permute-start(f32[104,128]{1,0:T(8,128)S(1)} %get-tuple-element.35), channel_id=1, source_target_pairs={{0,4},{4,0},{1,5},{5,1},{2,6},{6,2},{3,7},{7,3},{8,12},{12,8},{9,1... | collective-permute-start | bytes 159752 | tf_op jit(solution)/shard_map/ppermute | solution.py:677
  16.6 4.4 %collective-permute-start.4 = (f32[136,128]{1,0:T(8,128)S(1)}, f32[136,128]{1,0:T(8,128)S(1)}, u32[]{:S(2)}, u32[]{:S(2)}) collective-permute-start(f32[136,128]{1,0:T(8,128)S(1)} %get-tuple-element.41), channel_id=1, source_target_pairs={{0,8},{16,24},{8,0},{24,16},{1,9},{17,25},{9,1},{25,17},{2,10},{18... | collective-permute-start | bytes 208904 | tf_op jit(solution)/shard_map/ppermute | solution.py:677
  18.1 2.8 %collective-permute-start.5 = (f32[136,128]{1,0:T(8,128)S(1)}, f32[136,128]{1,0:T(8,128)S(1)}, u32[]{:S(2)}, u32[]{:S(2)}) collective-permute-start(f32[136,128]{1,0:T(8,128)S(1)} %get-tuple-element.42), channel_id=1, source_target_pairs={{8,16},{9,17},{10,18},{11,19},{16,8},{17,9},{18,10},{19,11},{0,1},... | collective-permute-start | bytes 208904 | tf_op jit(solution)/shard_map/ppermute | solution.py:677
  21.7 6.4 %collective-permute-start.6 = (f32[32,384]{1,0:T(8,128)S(1)}, f32[32,384]{1,0:T(8,128)S(1)}, u32[]{:S(2)}, u32[]{:S(2)}) collective-permute-start(f32[32,384]{1,0:T(8,128)S(1)} %get-tuple-element.44), channel_id=1, source_target_pairs={{0,1},{1,2},{2,3},{3,0},{4,5},{5,6},{6,7},{7,4},{8,9},{9,10},{10,1... | collective-permute-start | bytes 147464 | tf_op jit(solution)/shard_map/ppermute | solution.py:733
  21.8 6.3 %collective-permute-start.7 = (f32[32,384]{1,0:T(8,128)S(1)}, f32[32,384]{1,0:T(8,128)S(1)}, u32[]{:S(2)}, u32[]{:S(2)}) collective-permute-start(f32[32,384]{1,0:T(8,128)S(1)} %get-tuple-element.45), channel_id=1, source_target_pairs={{0,2},{1,3},{2,0},{3,1},{4,6},{5,7},{6,4},{7,5},{8,10},{9,11},{10,... | collective-permute-start | bytes 147464 | tf_op jit(solution)/shard_map/ppermute | solution.py:733
  24.5 3.6 %collective-permute-start.8 = (f32[32,384]{1,0:T(8,128)S(1)}, f32[32,384]{1,0:T(8,128)S(1)}, u32[]{:S(2)}, u32[]{:S(2)}) collective-permute-start(f32[32,384]{1,0:T(8,128)S(1)} %get-tuple-element.46), channel_id=1, source_target_pairs={{0,3},{1,0},{2,1},{3,2},{4,7},{5,4},{6,5},{7,6},{8,11},{9,8},{10,9... | collective-permute-start | bytes 147464 | tf_op jit(solution)/shard_map/ppermute | solution.py:733

commit v3 on v2

--- a/solution.py
+++ b/solution.py
@@ -109,7 +109,7 @@
 
 
 def pre_kernel(plan, count_ref, corner_hbm, fine_hbm, coarse_hbm, rhs, pre_ref, blk, *rest):
-    msg_refs, (res, corner_ref, sems) = rest[:-3], rest[-3:]
+    msg_refs, (corner_ref, sems) = rest[:-2], rest[-2:]
     pe, foot, tiles, slots = plan.pe, plan.foot, plan.tiles, plan.slots
     copies = [
         pltpu.make_async_copy(
@@ -129,48 +129,45 @@
     zero_gaps(pre_ref, plan)
     source, target = iota((4 * LANES, LANES), 0), iota((4 * LANES, LANES), 1)
     place = (source // LANES) * 32 + (source % LANES) // 64 * 16 + source % 32 // 2
-    table = jnp.where(place == target, 0.5, 0.0).astype(BF16)
+    summed = jnp.where(place == target, 0.5, 0.0)
+    source, target = iota((6 * LANES, LANES), 0), iota((6 * LANES, LANES), 1)
+    dy = source // 32 - 4 - 2 * (target // foot)
+    dz = source % 32 - 2 * (target % foot)
+    y_in, z_in = (dy >= 0) & (dy <= 1), (dz >= 0) & (dz <= 1)
+    weight = jnp.where(y_in & (dz >= -1) & (dz <= 2), 0.5, 0.0) + jnp.where(z_in & (dy >= -1) & (dy <= 2), 0.5, 0.0)
+    weight = jnp.where(y_in & z_in, -1.5, weight)
+    table = jnp.concatenate([summed, weight], 0).astype(BF16)
+    for copy in copies:
+        copy.wait()
+
+    lines = []
     for p in range(slots):
-        for copy in copies[p * tiles : (p + 1) * tiles]:
-            copy.wait()
         start = SUB + p * plan.fpitch
         for j in range(pe // SUB):
             rows = pl.ds(start + j * SUB, SUB)
-            values = []
             for t in range(tiles):
                 mid, total = fine_neighbors(rhs, t, start + j * SUB, tiles)
-                values.append(0.165 * mid + 0.0225 * total)
-            for t, v in enumerate(values):
-                pre_ref[t, rows, :] = v
-        for j in range(pe // SUB):
-            rows = pl.ds(start + j * SUB, SUB)
-            values = []
-            for t in range(tiles):
-                mid, total = fine_neighbors(pre_ref, t, start + j * SUB, tiles)
-                values.append(rhs[t, rows, :] - (6.0 * mid - total))
-            for t, v in enumerate(values):
-                res[t, rows, :] = v
-        lines = []
-        for half in range(2):
-            cols = []
-            for k in range(4):
-                t = 4 * half + k
-                cols.append(
-                    res[t, pl.ds(start, foot, stride=2), :]
-                    + res[t, pl.ds(start + 1, foot, stride=2), :]
-                )
-            lines.append(jnp.concatenate(cols, 1))
-        value = dot2(jnp.concatenate(lines, 0), table)
-        for ref in msg_refs:
-            ref[pl.ds(p * 2 * foot, 2 * foot), :] = value
-    for copy in copies[at:]:
-        copy.wait()
+                pre_ref[t, rows, :] = 0.165 * mid + 0.0225 * total
+
+        def every(ref, t, at):
+            return ref[t, pl.ds(start + at, foot, stride=2), :]
+
+        outer, inner = [], [jnp.zeros((foot, LANES), F32)]
+        for t in range(tiles):
+            outer.append(every(rhs, t, 0) + every(rhs, t, 1) + (every(pre_ref, t, -1) + every(pre_ref, t, 2)))
+            inner.append(every(pre_ref, t, 0) + every(pre_ref, t, 1))
+        inner.append(inner[0])
+        for first in range(0, tiles, 4):
+            lines.append(jnp.concatenate(outer[first : first + 4] + inner[first : first + 6], 1))
     lane = iota((SUB, LANES), 1)
     tags = jnp.zeros((SUB, LANES), F32)
     for p in range(slots):
         code = patch_code(plan, count_ref[0], corner_ref, p)
         tags = jnp.where(lane == p, code.astype(F32), tags)
     high, low = pack_faces(blk, plan)
+    value = dot2(jnp.concatenate(lines, 0), table)
+    for ref in msg_refs:
+        ref[pl.ds(0, plan.avg_rows), :] = value
     for shift, ref in enumerate(msg_refs, 1):
         at = plan.avg_rows
         ref[pl.ds(at, SUB), :] = tags
@@ -249,15 +246,11 @@
     lax.fori_loop(0, plan.slots * (plan.pe // SUB), rows8, 0)
 
 
-def late_step(plan, rhs, source, after, target):
-    del after
-    fixed_step(plan, rhs, source, target)
-
-
-def base_kernel(plan, blk, own_ref, rhs, pre_ref, comp, fixed):
+def base_kernel(plan, blk, own_ref, rhs, pre_ref, comp, fixed, work):
     codes = [message_code(plan, own_ref, p) for p in range(plan.slots)]
-    zero_gaps(fixed, plan)
-    fixed_step(plan, rhs, pre_ref, fixed)
+    zero_gaps(work, plan)
+    fixed_step(plan, rhs, pre_ref, work)
+    fixed_step(plan, rhs, work, fixed)
     cx, cy = plan.cx, plan.cy
     end = SUB + RIM * plan.pitch
     for base in (0, plan.crows):
@@ -586,33 +579,40 @@
     around = 3.0 * up + jnp.where(source == side_y, 1.0, 0.0) + jnp.where(source == side_z, 1.0, 0.0)
     zface = jnp.where((source == side_z) & ((fz == 0) | (fz == pe - 1)), 1.0, 0.0)
     table = jnp.concatenate([up, around, zface], 1).astype(BF16)
-    work = [lanes_from(got, 2 * t * win) for got in cuts for t in range(tiles)]
-    spread = dot2(jnp.concatenate(work, 0), table)
     low_y = jnp.where((target >= LANES - 32) & (source == fz // 2 + 1), 1.0, 0.0)
     high_y = jnp.where((target < 32) & (source == 3 * win + fz // 2 + 1), 1.0, 0.0)
-    ends = [lanes_from(got, 0) for got in cuts], [lanes_from(got, 2 * (tiles - 1) * win) for got in cuts]
-    lows = dot2(jnp.concatenate(ends[0], 0), low_y.astype(BF16))
-    highs = dot2(jnp.concatenate(ends[1], 0), high_y.astype(BF16))
+    low_y, high_y = low_y.astype(BF16), high_y.astype(BF16)
     xsel = jnp.where((source == fz // 2), 1.0, 0.0).astype(BF16)
-    xfaces = dot2(
-        jnp.concatenate([lanes_from(got, plan.elow + i * foot) for got in cuts for i in range(2)], 0), xsel
-    )
+
+    def products(got):
+        work = [lanes_from(got, 2 * t * win) for t in range(tiles)]
+        sides = [lanes_from(got, plan.elow + i * foot) for i in range(2)]
+        return (
+            dot2(jnp.concatenate(work, 0), table),
+            dot2(work[0], low_y),
+            dot2(work[tiles - 1], high_y),
+            dot2(jnp.concatenate(sides, 0), xsel),
+        )
+
+    ahead = products(cuts[0])
     lane1 = iota((1, LANES), 1)
     copies = [pltpu.make_async_copy(out_ref.at[p], out_hbm.at[p], sems.at[p]) for p in range(slots)]
     lane = iota((SUB, LANES), 1)
     for p in range(slots):
         start = SUB + p * plan.fpitch
         ustart = SUB + p * (foot + SUB)
-        for v, k in ((lows, 0), (highs, 1)):
-            line = v[p * foot : (p + 1) * foot]
+        spread, lows, highs, xfaces = ahead
+        if p + 1 < slots:
+            ahead = products(cuts[p + 1])
+        for k, line in enumerate((lows, highs)):
             for parity in range(2):
                 yghost[k, pl.ds(start + parity, foot, stride=2), :] = line
         for t in range(tiles):
-            block = spread[(p * tiles + t) * foot : (p * tiles + t + 1) * foot]
+            block = spread[t * foot : (t + 1) * foot]
             mine = block[:, 0:LANES]
             ups[t, pl.ds(ustart, foot), :] = mine
             for i, (urow, row) in enumerate(((ustart - 1, start - 1), (ustart + foot, start + pe))):
-                face = xfaces[(2 * p + i) * foot : (2 * p + i + 1) * foot]
+                face = xfaces[i * foot : (i + 1) * foot]
                 line = jnp.where(lane1 < 64, face[2 * t : 2 * t + 1], face[2 * t + 1 : 2 * t + 2])
                 ups[t, pl.ds(urow, 1), :] = line
                 first[t, pl.ds(row, 1), :] = line
@@ -697,7 +697,7 @@
             pltpu.with_memory_space_constraint(a, pltpu.HBM)
             for a in (patch_corner, fine_rhs, coarse_rhs.reshape(block_shape))
         ],
-        scratch=(fine_shape, pltpu.VMEM(patch_corner.shape, jnp.int32)),
+        scratch=(pltpu.VMEM(patch_corner.shape, jnp.int32),),
         smem=1,
         hbm_in=3,
         sems=plan.slots * plan.tiles + 2,
@@ -710,7 +710,9 @@
     msgs = []
     for s, m in zip(shifts, sends):
         msgs.append(lax.ppermute(m, "gz", ring(s)))
-    comp, fixed = call(bind(base_kernel, plan), [comp_shape, fine_shape], (block, own, rhs, pre), cost=4 << 20)
+    comp, fixed = call(
+        bind(base_kernel, plan), [comp_shape, fine_shape], (block, own, rhs, pre), scratch=(fine_shape,), cost=4 << 20
+    )
     comp, *ysends = call(bind(compose_kernel, plan), [comp_shape] + [yshape] * n_y, (comp, own, *msgs), aliases={0: 0})
     ygot = swap_pairs("gy", plan.ny, ysends)
     second, third = call(bind(inner_kernel, plan), [comp_shape, third_shape], (comp,), cost=4 << 20)
@@ -732,8 +734,6 @@
     )
     back = [cuts[0]] + [lax.ppermute(cuts[s], "gz", ring(s)) for s in shifts]
     (out,) = call(bind(emit_kernel, plan), [block_shape], (third,), cost=2 << 20)
-    tiny = lax.slice_in_dim(cuts[0], 0, SUB, axis=0)
-    (fixed,) = call(bind(late_step, plan), [fine_shape], (rhs, fixed, tiny), cost=4 << 20)
     (fine,) = call(
         bind(post_kernel, plan),
         [fine_rhs.shape],

time: 29.9 us -> 29.3 us (0.980)
  the two profiles are of different devices: /device:TPU:0 before, /device:TPU:13 now
where the time goes in v3:
time: 29.3 us; the launch traced here: 29.1 us
  Pallas kernels  13.9 us (47%)
  starting transfers between devices  10.2 us (35%)
  waiting for transfers between devices  3.59 us (12%)
  between operations  1.37 us (5%)
    pallas_call x9, Pallas kernels, call(): pl.pallas_call(kernel, out_shape=[jax.ShapeDtypeStruct(s, F32) for s in o...  13.9 us
    ppermute x3, starting transfers between devices, cycle(): back = [cuts[0]] + [lax.ppermute(cuts[s], 'gz', ring(s)) for s in shifts]  4.08 us
    ppermute x3, starting transfers between devices, swap_pairs(): got.append(lax.ppermute(send, names, pairs))  4.02 us
    ppermute x3, waiting for transfers between devices, cycle(): back = [cuts[0]] + [lax.ppermute(cuts[s], 'gz', ring(s)) for s in shifts]  2.68 us
    ppermute x3, starting transfers between devices, cycle(): msgs.append(lax.ppermute(m, 'gz', ring(s)))  2.14 us
    ppermute x3, waiting for transfers between devices, cycle(): msgs.append(lax.ppermute(m, 'gz', ring(s)))  0.9 us
  transfers between devices with their start and end apart: 9, of which 3 were waited for; matrix products, arithmetic and copies ran while one was open for 0% of the time, Pallas kernels for 30%

profile of v3, /device:TPU:13, one launch (start us, length us, event | category | flops | bytes accessed | tf_op | source)
XLA Modules:
  0.0 29.1 jit_solution(18252628936068467178)
XLA Ops:
  1.3 2.3 %shard_map.59 = (f32[8,128,128]{2,1,0:T(8,128)S(1)}, f32[8,128,128]{2,1,0:T(8,128)S(1)}, f32[1024,128]{1,0:T(8,128)S(1)}, f32[136,128]{1,0:T(8,128)S(1)}, f32[10...) custom-call(s32[1]{0:T(128)S(6)} %copy.22.count_ref, s32[3,3]{1,0:T(4,128)} %corner_hbm.1, f32[3,32,1024]{2,1,0:T(8,128)} %fine_hbm.1, ...), custom_call_target="tpu_custom_call" | custom-call | tf_op jit(solution)/shard_map/pallas_call | solution.py:654
  3.6 0.7 %collective-permute-start.2 = (f32[136,128]{1,0:T(8,128)S(1)}, f32[136,128]{1,0:T(8,128)S(1)}, u32[]{:S(2)}, u32[]{:S(2)}) collective-permute-start(f32[136,128]{1,0:T(8,128)S(1)} %get-tuple-element.32), channel_id=1, source_target_pairs={{0,3},{1,0},{2,1},{3,2},{4,7},{5,4},{6,5},{7,6},{8,11},{9,8},{10,9... | collective-permute-start | bytes 208904 | tf_op jit(solution)/shard_map/ppermute | solution.py:712
  4.3 1.1 %collective-permute-start = (f32[136,128]{1,0:T(8,128)S(1)}, f32[136,128]{1,0:T(8,128)S(1)}, u32[]{:S(2)}, u32[]{:S(2)}) collective-permute-start(f32[136,128]{1,0:T(8,128)S(1)} %get-tuple-element.25.own_ref), channel_id=1, source_target_pairs={{0,1},{1,2},{2,3},{3,0},{4,5},{5,6},{6,7},{7,4},{8,9},{9,10},{10,1... | collective-permute-start | bytes 208904 | tf_op jit(solution)/shard_map/ppermute | solution.py:712
  5.4 0.3 %collective-permute-start.1 = (f32[104,128]{1,0:T(8,128)S(1)}, f32[104,128]{1,0:T(8,128)S(1)}, u32[]{:S(2)}, u32[]{:S(2)}) collective-permute-start(f32[104,128]{1,0:T(8,128)S(1)} %get-tuple-element.31), channel_id=1, source_target_pairs={{0,2},{1,3},{2,0},{3,1},{4,6},{5,7},{6,4},{7,5},{8,10},{9,11},{10,... | collective-permute-start | bytes 159752 | tf_op jit(solution)/shard_map/ppermute | solution.py:712
  5.7 2.9 %shard_map.60 = (f32[3072,128]{1,0:T(8,128)S(1)}, f32[8,128,128]{2,1,0:T(8,128)S(1)}) custom-call(f32[1024,128]{1,0:T(8,128)S(1)} %get-tuple-element.26.blk, f32[136,128]{1,0:T(8,128)S(1)} %get-tuple-element.25.own_ref, f32[8,128,128]{2,1,0:T(8,128)S(1)} %get-tuple-element.27.rhs, f32[8,128,128]{2,1,0:T(8,128)S(1)} %get-tuple-element.28.pre_ref), custom_call_target="tpu_custom_call" | custom-call | flops 4194304 | bytes 4194304 | tf_op jit(solution)/shard_map/pallas_call | solution.py:654
  8.6 0.9 %collective-permute-done.1.rest_1_.rest_3_ = f32[104,128]{1,0:T(8,128)S(1)} collective-permute-done((f32[104,128]{1,0:T(8,128)S(1)}, f32[104,128]{1,0:T(8,128)S(1)}, u32[]{:S(2)}, u32[]{:S(2)}) %collective-permute-start.1) | collective-permute-done | bytes 53280 | tf_op jit(solution)/shard_map/ppermute | solution.py:712
  9.5 0.0 collective-permute-done.2.rest_2_.rest_4_
  9.5 0.0 collective-permute-done.rest_0_.rest_2_
  9.5 0.6 %shard_map.61 = (f32[3072,128]{1,0:T(8,128)S(1)}, f32[104,128]{1,0:T(8,128)S(1)}) custom-call(f32[3072,128]{1,0:T(8,128)S(1)} %get-tuple-element.30.comp_in, f32[136,128]{1,0:T(8,128)S(1)} %get-tuple-element.25.own_ref, f32[136,128]{1,0:T(8,128)S(1)} %collective-permute-done.rest_0_.rest_2_, ...), custom_call_target="tpu_custom_call", output_to_operand_aliasing={{0}: (0, {})} | custom-call | tf_op jit(solution)/shard_map/pallas_call | solution.py:654
  10.1 1.9 %collective-permute-start.3 = (f32[104,128]{1,0:T(8,128)S(1)}, f32[104,128]{1,0:T(8,128)S(1)}, u32[]{:S(2)}, u32[]{:S(2)}) collective-permute-start(f32[104,128]{1,0:T(8,128)S(1)} %get-tuple-element.35), channel_id=1, source_target_pairs={{0,4},{4,0},{1,5},{5,1},{2,6},{6,2},{3,7},{7,3},{8,12},{12,8},{9,1... | collective-permute-start | bytes 159752 | tf_op jit(solution)/shard_map/ppermute | solution.py:677
  12.0 2.9 %shard_map.62 = (f32[3072,128]{1,0:T(8,128)S(1)}, f32[4608,128]{1,0:T(8,128)S(1)}) custom-call(f32[3072,128]{1,0:T(8,128)S(1)} %get-tuple-element.33.comp.comp_in), custom_call_target="tpu_custom_call" | custom-call | flops 4194304 | bytes 4194304 | tf_op jit(solution)/shard_map/pallas_call | solution.py:654
  14.9 0.0 collective-permute-done.3.rest_0_
  14.9 0.2 shard_map.63
  15.1 0.1 collective-permute-start.4
  15.1 2.0 %collective-permute-start.5 = (f32[136,128]{1,0:T(8,128)S(1)}, f32[136,128]{1,0:T(8,128)S(1)}, u32[]{:S(2)}, u32[]{:S(2)}) collective-permute-start(f32[136,128]{1,0:T(8,128)S(1)} %get-tuple-element.42), channel_id=1, source_target_pairs={{8,16},{9,17},{10,18},{11,19},{16,8},{17,9},{18,10},{19,11},{0,1},... | collective-permute-start | bytes 208904 | tf_op jit(solution)/shard_map/ppermute | solution.py:677
  17.2 2.2 %shard_map.64 = (f32[3072,128]{1,0:T(8,128)S(1)}, f32[4608,128]{1,0:T(8,128)S(1)}) custom-call(f32[3072,128]{1,0:T(8,128)S(1)} %get-tuple-element.36.comp.comp_in, f32[3072,128]{1,0:T(8,128)S(1)} %get-tuple-element.37.second_in, f32[4608,128]{1,0:T(8,128)S(1)} %get-tuple-element.38.third_in), custom_call_target="tpu_custom_call", output_to_operand_aliasing={{0}: (1, {}), {1}: (2, {})} | custom-call | flops 8388608 | bytes 8388608 | tf_op jit(solution)/shard_map/pallas_call | solution.py:654
  19.3 0.0 collective-permute-done.4.rest_0_
  19.3 0.6 %shard_map.65 = (f32[3072,128]{1,0:T(8,128)S(1)}, f32[3072,128]{1,0:T(8,128)S(1)}, f32[4608,128]{1,0:T(8,128)S(1)}, f32[32,384]{1,0:T(8,128)S(1)}, f32[32,384]{1...) custom-call(f32[3072,128]{1,0:T(8,128)S(1)} %get-tuple-element.36.co, ...), custom_call_target="tpu_custom_call", output_to_operand_aliasing={{0}: (0, {}), {1}: (1, {}), {2}: (2, {})} | custom-call | tf_op jit(solution)/shard_map/pallas_call | solution.py:654
  20.0 1.8 %collective-permute-start.6 = (f32[32,384]{1,0:T(8,128)S(1)}, f32[32,384]{1,0:T(8,128)S(1)}, u32[]{:S(2)}, u32[]{:S(2)}) collective-permute-start(f32[32,384]{1,0:T(8,128)S(1)} %get-tuple-element.44), channel_id=1, source_target_pairs={{0,1},{1,2},{2,3},{3,0},{4,5},{5,6},{6,7},{7,4},{8,9},{9,10},{10,1... | collective-permute-start | bytes 147464 | tf_op jit(solution)/shard_map/ppermute | solution.py:735
  21.7 2.3 %collective-permute-start.7 = (f32[32,384]{1,0:T(8,128)S(1)}, f32[32,384]{1,0:T(8,128)S(1)}, u32[]{:S(2)}, u32[]{:S(2)}) collective-permute-start(f32[32,384]{1,0:T(8,128)S(1)} %get-tuple-element.45), channel_id=1, source_target_pairs={{0,2},{1,3},{2,0},{3,1},{4,6},{5,7},{6,4},{7,5},{8,10},{9,11},{10,... | collective-permute-start | bytes 147464 | tf_op jit(solution)/shard_map/ppermute | solution.py:735
  24.0 0.8 %shard_map.67 = f32[1024,128]{1,0:T(8,128)} custom-call(f32[4608,128]{1,0:T(8,128)S(1)} %get-tuple-element.47.third), custom_call_target="tpu_custom_call" | custom-call | flops 2097152 | bytes 2097152 | tf_op jit(solution)/shard_map/pallas_call | solution.py:654
  24.9 1.9 %collective-permute-done.7.rest_2_ = f32[32,384]{1,0:T(8,128)S(1)} collective-permute-done((f32[32,384]{1,0:T(8,128)S(1)}, f32[32,384]{1,0:T(8,128)S(1)}, u32[]{:S(2)}, u32[]{:S(2)}) %collective-permute-start.7) | collective-permute-done | bytes 49184 | tf_op jit(solution)/shard_map/ppermute | solution.py:735
  26.7 0.8 %collective-permute-done.8.rest_3_ = f32[32,384]{1,0:T(8,128)S(1)} collective-permute-done((f32[32,384]{1,0:T(8,128)S(1)}, f32[32,384]{1,0:T(8,128)S(1)}, u32[]{:S(2)}, u32[]{:S(2)}) %collective-permute-start.8) | collective-permute-done | bytes 49184 | tf_op jit(solution)/shard_map/ppermute | solution.py:735
  27.5 1.6 %shard_map.66 = f32[3,32,1024]{2,1,0:T(8,128)} custom-call(f32[136,128]{1,0:T(8,128)S(1)} %get-tuple-element.25.own_ref, f32[8,128,128]{2,1,0:T(8,128)S(1)} %get-tuple-element.29.fixed, f32[32,384]{1,0:T(8,128)S(1)} %get-tuple-element.43.rest_0_, f32[32,384]{1,0:T(8,128)S(1)} %collective-permute-done.6.rest_1_, ...), custom_call_target="tpu_custom_call" | custom-call | tf_op jit(solution)/shard_map/pallas_call | solution.py:654
  (3 shorter events, 0.0 us)
Async XLA Ops:
  3.6 5.9 %collective-permute-start.2 = (f32[136,128]{1,0:T(8,128)S(1)}, f32[136,128]{1,0:T(8,128)S(1)}, u32[]{:S(2)}, u32[]{:S(2)}) collective-permute-start(f32[136,128]{1,0:T(8,128)S(1)} %get-tuple-element.32), channel_id=1, source_target_pairs={{0,3},{1,0},{2,1},{3,2},{4,7},{5,4},{6,5},{7,6},{8,11},{9,8},{10,9... | collective-permute-start | bytes 208904 | tf_op jit(solution)/shard_map/ppermute | solution.py:712
  4.3 5.2 %collective-permute-start = (f32[136,128]{1,0:T(8,128)S(1)}, f32[136,128]{1,0:T(8,128)S(1)}, u32[]{:S(2)}, u32[]{:S(2)}) collective-permute-start(f32[136,128]{1,0:T(8,128)S(1)} %get-tuple-element.25.own_ref), channel_id=1, source_target_pairs={{0,1},{1,2},{2,3},{3,0},{4,5},{5,6},{6,7},{7,4},{8,9},{9,10},{10,1... | collective-permute-start | bytes 208904 | tf_op jit(solution)/shard_map/ppermute | solution.py:712
  5.4 4.1 %collective-permute-start.1 = (f32[104,128]{1,0:T(8,128)S(1)}, f32[104,128]{1,0:T(8,128)S(1)}, u32[]{:S(2)}, u32[]{:S(2)}) collective-permute-start(f32[104,128]{1,0:T(8,128)S(1)} %get-tuple-element.31), channel_id=1, source_target_pairs={{0,2},{1,3},{2,0},{3,1},{4,6},{5,7},{6,4},{7,5},{8,10},{9,11},{10,... | collective-permute-start | bytes 159752 | tf_op jit(solution)/shard_map/ppermute | solution.py:712
  10.1 4.8 %collective-permute-start.3 = (f32[104,128]{1,0:T(8,128)S(1)}, f32[104,128]{1,0:T(8,128)S(1)}, u32[]{:S(2)}, u32[]{:S(2)}) collective-permute-start(f32[104,128]{1,0:T(8,128)S(1)} %get-tuple-element.35), channel_id=1, source_target_pairs={{0,4},{4,0},{1,5},{5,1},{2,6},{6,2},{3,7},{7,3},{8,12},{12,8},{9,1... | collective-permute-start | bytes 159752 | tf_op jit(solution)/shard_map/ppermute | solution.py:677
  15.1 4.3 %collective-permute-start.4 = (f32[136,128]{1,0:T(8,128)S(1)}, f32[136,128]{1,0:T(8,128)S(1)}, u32[]{:S(2)}, u32[]{:S(2)}) collective-permute-start(f32[136,128]{1,0:T(8,128)S(1)} %get-tuple-element.41), channel_id=1, source_target_pairs={{0,8},{16,24},{8,0},{24,16},{1,9},{17,25},{9,1},{25,17},{2,10},{18... | collective-permute-start | bytes 208904 | tf_op jit(solution)/shard_map/ppermute | solution.py:677
  15.1 4.2 %collective-permute-start.5 = (f32[136,128]{1,0:T(8,128)S(1)}, f32[136,128]{1,0:T(8,128)S(1)}, u32[]{:S(2)}, u32[]{:S(2)}) collective-permute-start(f32[136,128]{1,0:T(8,128)S(1)} %get-tuple-element.42), channel_id=1, source_target_pairs={{8,16},{9,17},{10,18},{11,19},{16,8},{17,9},{18,10},{19,11},{0,1},... | collective-permute-start | bytes 208904 | tf_op jit(solution)/shard_map/ppermute | solution.py:677
  20.0 4.9 %collective-permute-start.6 = (f32[32,384]{1,0:T(8,128)S(1)}, f32[32,384]{1,0:T(8,128)S(1)}, u32[]{:S(2)}, u32[]{:S(2)}) collective-permute-start(f32[32,384]{1,0:T(8,128)S(1)} %get-tuple-element.44), channel_id=1, source_target_pairs={{0,1},{1,2},{2,3},{3,0},{4,5},{5,6},{6,7},{7,4},{8,9},{9,10},{10,1... | collective-permute-start | bytes 147464 | tf_op jit(solution)/shard_map/ppermute | solution.py:735
  21.7 5.0 %collective-permute-start.7 = (f32[32,384]{1,0:T(8,128)S(1)}, f32[32,384]{1,0:T(8,128)S(1)}, u32[]{:S(2)}, u32[]{:S(2)}) collective-permute-start(f32[32,384]{1,0:T(8,128)S(1)} %get-tuple-element.45), channel_id=1, source_target_pairs={{0,2},{1,3},{2,0},{3,1},{4,6},{5,7},{6,4},{7,5},{8,10},{9,11},{10,... | collective-permute-start | bytes 147464 | tf_op jit(solution)/shard_map/ppermute | solution.py:735
  24.0 3.5 %collective-permute-start.8 = (f32[32,384]{1,0:T(8,128)S(1)}, f32[32,384]{1,0:T(8,128)S(1)}, u32[]{:S(2)}, u32[]{:S(2)}) collective-permute-start(f32[32,384]{1,0:T(8,128)S(1)} %get-tuple-element.46), channel_id=1, source_target_pairs={{0,3},{1,0},{2,1},{3,2},{4,7},{5,4},{6,5},{7,6},{8,11},{9,8},{10,9... | collective-permute-start | bytes 147464 | tf_op jit(solution)/shard_map/ppermute | solution.py:735

commit v4 on v3

--- a/solution.py
+++ b/solution.py
@@ -419,7 +419,7 @@
 
 def inner_kernel(plan, comp, second, third):
     s = Sweeps(plan, comp, second, third)
-    s.planes(s.step2, 1, plan.cx - 2, range(s.main))
+    s.planes(s.step2, 1, plan.cx - 2, range(s.main), group=3)
     s.planes(s.step3, 2, plan.cx - 3, range(1, s.main - 1))
 
 
@@ -432,7 +432,7 @@
             rims = pl.ds(base + plan.row(0, rim), plan.cx, stride=plan.pitch)
             second[rows, :] = second[rows, :] + 0.0225 * comp[rims, :]
     s.planes(s.step2, 0, plan.cx - 2, (s.main,), group=4)
-    s.planes(s.step3, 2, plan.cx - 3, (0, s.main - 1, s.main))
+    s.planes(s.step3, 2, plan.cx - 3, (0, s.main - 1, s.main), group=4)
 
 
 def put_xfaces(plan, x_refs, comp):
@@ -732,7 +732,9 @@
         (comp, second, third, own, *xgot, *msgs),
         aliases={0: 0, 1: 1, 2: 2},
     )
-    back = [cuts[0]] + [lax.ppermute(cuts[s], "gz", ring(s)) for s in shifts]
+    back = [cuts[0]]
+    for s in shifts:
+        back.append(lax.ppermute(cuts[s], "gz", ring(s)))
     (out,) = call(bind(emit_kernel, plan), [block_shape], (third,), cost=2 << 20)
     (fine,) = call(
         bind(post_kernel, plan),

time: 29.3 us -> 28.9 us (0.986)
  Pallas kernels: 13.9 us -> 13 us
  waiting for transfers between devices: 3.59 us -> 3.92 us
    pallas_call x9, Pallas kernels: 13.9 us -> 13 us  [call(): pl.pallas_call(kernel, out_shape=[jax.ShapeDtypeStruct(s, F32) for s in o...]
    ppermute x3, waiting for transfers between devices: 0.01 us -> 0.34 us  [swap_pairs(): got.append(lax.ppermute(send, names, pairs))]
  transfers between devices with their start and end apart: 9 -> 9, of which waited for: 3 -> 4; matrix products, arithmetic and copies ran while one was open for 0% -> 0% of each run, Pallas kernels for 30% -> 27%
where the time goes in v4:
time: 28.9 us; the launch traced here: 28.8 us
  Pallas kernels  13 us (45%)
  starting transfers between devices  10.4 us (36%)
  waiting for transfers between devices  3.92 us (14%)
  between operations  1.36 us (5%)
    pallas_call x9, Pallas kernels, call(): pl.pallas_call(kernel, out_shape=[jax.ShapeDtypeStruct(s, F32) for s in o...  13 us
    ppermute x3, starting transfers between devices, cycle(): back.append(lax.ppermute(cuts[s], 'gz', ring(s)))  4.28 us
    ppermute x3, starting transfers between devices, swap_pairs(): got.append(lax.ppermute(send, names, pairs))  4.02 us
    ppermute x3, waiting for transfers between devices, cycle(): back.append(lax.ppermute(cuts[s], 'gz', ring(s)))  2.68 us
    ppermute x3, starting transfers between devices, cycle(): msgs.append(lax.ppermute(m, 'gz', ring(s)))  2.14 us
    ppermute x3, waiting for transfers between devices, cycle(): msgs.append(lax.ppermute(m, 'gz', ring(s)))  0.9 us
  transfers between devices with their start and end apart: 9, of which 4 were waited for; matrix products, arithmetic and copies ran while one was open for 0% of the time, Pallas kernels for 27%

profile of v4, /device:TPU:13, one launch (start us, length us, event | category | flops | bytes accessed | tf_op | source)
XLA Modules:
  0.0 28.8 jit_solution(11225494574974355116)
XLA Ops:
  1.3 2.3 %shard_map.59 = (f32[8,128,128]{2,1,0:T(8,128)S(1)}, f32[8,128,128]{2,1,0:T(8,128)S(1)}, f32[1024,128]{1,0:T(8,128)S(1)}, f32[136,128]{1,0:T(8,128)S(1)}, f32[10...) custom-call(s32[1]{0:T(128)S(6)} %copy.22.count_ref, s32[3,3]{1,0:T(4,128)} %corner_hbm.1, f32[3,32,1024]{2,1,0:T(8,128)} %fine_hbm.1, ...), custom_call_target="tpu_custom_call" | custom-call | tf_op jit(solution)/shard_map/pallas_call | solution.py:654
  3.6 0.7 %collective-permute-start.2 = (f32[136,128]{1,0:T(8,128)S(1)}, f32[136,128]{1,0:T(8,128)S(1)}, u32[]{:S(2)}, u32[]{:S(2)}) collective-permute-start(f32[136,128]{1,0:T(8,128)S(1)} %get-tuple-element.32), channel_id=1, source_target_pairs={{0,3},{1,0},{2,1},{3,2},{4,7},{5,4},{6,5},{7,6},{8,11},{9,8},{10,9... | collective-permute-start | bytes 208904 | tf_op jit(solution)/shard_map/ppermute | solution.py:712
  4.3 1.1 %collective-permute-start = (f32[136,128]{1,0:T(8,128)S(1)}, f32[136,128]{1,0:T(8,128)S(1)}, u32[]{:S(2)}, u32[]{:S(2)}) collective-permute-start(f32[136,128]{1,0:T(8,128)S(1)} %get-tuple-element.25.own_ref), channel_id=1, source_target_pairs={{0,1},{1,2},{2,3},{3,0},{4,5},{5,6},{6,7},{7,4},{8,9},{9,10},{10,1... | collective-permute-start | bytes 208904 | tf_op jit(solution)/shard_map/ppermute | solution.py:712
  5.4 0.3 %collective-permute-start.1 = (f32[104,128]{1,0:T(8,128)S(1)}, f32[104,128]{1,0:T(8,128)S(1)}, u32[]{:S(2)}, u32[]{:S(2)}) collective-permute-start(f32[104,128]{1,0:T(8,128)S(1)} %get-tuple-element.31), channel_id=1, source_target_pairs={{0,2},{1,3},{2,0},{3,1},{4,6},{5,7},{6,4},{7,5},{8,10},{9,11},{10,... | collective-permute-start | bytes 159752 | tf_op jit(solution)/shard_map/ppermute | solution.py:712
  5.7 2.9 %shard_map.60 = (f32[3072,128]{1,0:T(8,128)S(1)}, f32[8,128,128]{2,1,0:T(8,128)S(1)}) custom-call(f32[1024,128]{1,0:T(8,128)S(1)} %get-tuple-element.26.blk, f32[136,128]{1,0:T(8,128)S(1)} %get-tuple-element.25.own_ref, f32[8,128,128]{2,1,0:T(8,128)S(1)} %get-tuple-element.27.rhs, f32[8,128,128]{2,1,0:T(8,128)S(1)} %get-tuple-element.28.pre_ref), custom_call_target="tpu_custom_call" | custom-call | flops 4194304 | bytes 4194304 | tf_op jit(solution)/shard_map/pallas_call | solution.py:654
  8.6 0.9 %collective-permute-done.1.rest_1_.rest_3_ = f32[104,128]{1,0:T(8,128)S(1)} collective-permute-done((f32[104,128]{1,0:T(8,128)S(1)}, f32[104,128]{1,0:T(8,128)S(1)}, u32[]{:S(2)}, u32[]{:S(2)}) %collective-permute-start.1) | collective-permute-done | bytes 53280 | tf_op jit(solution)/shard_map/ppermute | solution.py:712
  9.5 0.0 collective-permute-done.2.rest_2_.rest_4_
  9.5 0.0 collective-permute-done.rest_0_.rest_2_
  9.5 0.6 %shard_map.61 = (f32[3072,128]{1,0:T(8,128)S(1)}, f32[104,128]{1,0:T(8,128)S(1)}) custom-call(f32[3072,128]{1,0:T(8,128)S(1)} %get-tuple-element.30.comp_in, f32[136,128]{1,0:T(8,128)S(1)} %get-tuple-element.25.own_ref, f32[136,128]{1,0:T(8,128)S(1)} %collective-permute-done.rest_0_.rest_2_, ...), custom_call_target="tpu_custom_call", output_to_operand_aliasing={{0}: (0, {})} | custom-call | tf_op jit(solution)/shard_map/pallas_call | solution.py:654
  10.1 1.9 %collective-permute-start.3 = (f32[104,128]{1,0:T(8,128)S(1)}, f32[104,128]{1,0:T(8,128)S(1)}, u32[]{:S(2)}, u32[]{:S(2)}) collective-permute-start(f32[104,128]{1,0:T(8,128)S(1)} %get-tuple-element.35), channel_id=1, source_target_pairs={{0,4},{4,0},{1,5},{5,1},{2,6},{6,2},{3,7},{7,3},{8,12},{12,8},{9,1... | collective-permute-start | bytes 159752 | tf_op jit(solution)/shard_map/ppermute | solution.py:677
  12.0 2.5 %shard_map.62 = (f32[3072,128]{1,0:T(8,128)S(1)}, f32[4608,128]{1,0:T(8,128)S(1)}) custom-call(f32[3072,128]{1,0:T(8,128)S(1)} %get-tuple-element.33.comp.comp_in), custom_call_target="tpu_custom_call" | custom-call | flops 4194304 | bytes 4194304 | tf_op jit(solution)/shard_map/pallas_call | solution.py:654
  14.5 0.2 shard_map.63
  14.7 0.1 collective-permute-start.4
  14.8 2.0 %collective-permute-start.5 = (f32[136,128]{1,0:T(8,128)S(1)}, f32[136,128]{1,0:T(8,128)S(1)}, u32[]{:S(2)}, u32[]{:S(2)}) collective-permute-start(f32[136,128]{1,0:T(8,128)S(1)} %get-tuple-element.42), channel_id=1, source_target_pairs={{8,16},{9,17},{10,18},{11,19},{16,8},{17,9},{18,10},{19,11},{0,1},... | collective-permute-start | bytes 208904 | tf_op jit(solution)/shard_map/ppermute | solution.py:677
  16.8 1.6 %shard_map.64 = (f32[3072,128]{1,0:T(8,128)S(1)}, f32[4608,128]{1,0:T(8,128)S(1)}) custom-call(f32[3072,128]{1,0:T(8,128)S(1)} %get-tuple-element.36.comp.comp_in, f32[3072,128]{1,0:T(8,128)S(1)} %get-tuple-element.37.second_in, f32[4608,128]{1,0:T(8,128)S(1)} %get-tuple-element.38.third_in), custom_call_target="tpu_custom_call", output_to_operand_aliasing={{0}: (1, {}), {1}: (2, {})} | custom-call | flops 8388608 | bytes 8388608 | tf_op jit(solution)/shard_map/pallas_call | solution.py:654
  18.4 0.0 collective-permute-done.4.rest_0_
  18.5 0.3 %collective-permute-done.5.rest_1_ = f32[136,128]{1,0:T(8,128)S(1)} collective-permute-done((f32[136,128]{1,0:T(8,128)S(1)}, f32[136,128]{1,0:T(8,128)S(1)}, u32[]{:S(2)}, u32[]{:S(2)}) %collective-permute-start.5) | collective-permute-done | bytes 69664 | tf_op jit(solution)/shard_map/ppermute | solution.py:677
  18.8 0.6 %shard_map.65 = (f32[3072,128]{1,0:T(8,128)S(1)}, f32[3072,128]{1,0:T(8,128)S(1)}, f32[4608,128]{1,0:T(8,128)S(1)}, f32[32,384]{1,0:T(8,128)S(1)}, f32[32,384]{1...) custom-call(f32[3072,128]{1,0:T(8,128)S(1)} %get-tuple-element.36.co, ...), custom_call_target="tpu_custom_call", output_to_operand_aliasing={{0}: (0, {}), {1}: (1, {}), {2}: (2, {})} | custom-call | tf_op jit(solution)/shard_map/pallas_call | solution.py:654
  19.4 2.3 %collective-permute-start.6 = (f32[32,384]{1,0:T(8,128)S(1)}, f32[32,384]{1,0:T(8,128)S(1)}, u32[]{:S(2)}, u32[]{:S(2)}) collective-permute-start(f32[32,384]{1,0:T(8,128)S(1)} %get-tuple-element.44), channel_id=1, source_target_pairs={{0,1},{1,2},{2,3},{3,0},{4,5},{5,6},{6,7},{7,4},{8,9},{9,10},{10,1... | collective-permute-start | bytes 147464 | tf_op jit(solution)/shard_map/ppermute | solution.py:737
  21.7 1.9 %collective-permute-start.7 = (f32[32,384]{1,0:T(8,128)S(1)}, f32[32,384]{1,0:T(8,128)S(1)}, u32[]{:S(2)}, u32[]{:S(2)}) collective-permute-start(f32[32,384]{1,0:T(8,128)S(1)} %get-tuple-element.45), channel_id=1, source_target_pairs={{0,2},{1,3},{2,0},{3,1},{4,6},{5,7},{6,4},{7,5},{8,10},{9,11},{10,... | collective-permute-start | bytes 147464 | tf_op jit(solution)/shard_map/ppermute | solution.py:737
  23.7 0.8 %shard_map.67 = f32[1024,128]{1,0:T(8,128)} custom-call(f32[4608,128]{1,0:T(8,128)S(1)} %get-tuple-element.47.third), custom_call_target="tpu_custom_call" | custom-call | flops 2097152 | bytes 2097152 | tf_op jit(solution)/shard_map/pallas_call | solution.py:654
  24.5 1.9 %collective-permute-done.7.rest_2_ = f32[32,384]{1,0:T(8,128)S(1)} collective-permute-done((f32[32,384]{1,0:T(8,128)S(1)}, f32[32,384]{1,0:T(8,128)S(1)}, u32[]{:S(2)}, u32[]{:S(2)}) %collective-permute-start.7) | collective-permute-done | bytes 49184 | tf_op jit(solution)/shard_map/ppermute | solution.py:737
  26.4 0.8 %collective-permute-done.8.rest_3_ = f32[32,384]{1,0:T(8,128)S(1)} collective-permute-done((f32[32,384]{1,0:T(8,128)S(1)}, f32[32,384]{1,0:T(8,128)S(1)}, u32[]{:S(2)}, u32[]{:S(2)}) %collective-permute-start.8) | collective-permute-done | bytes 49184 | tf_op jit(solution)/shard_map/ppermute | solution.py:737
  27.2 1.6 %shard_map.66 = f32[3,32,1024]{2,1,0:T(8,128)} custom-call(f32[136,128]{1,0:T(8,128)S(1)} %get-tuple-element.25.own_ref, f32[8,128,128]{2,1,0:T(8,128)S(1)} %get-tuple-element.29.fixed, f32[32,384]{1,0:T(8,128)S(1)} %get-tuple-element.43.rest_0_, f32[32,384]{1,0:T(8,128)S(1)} %collective-permute-done.6.rest_1_, ...), custom_call_target="tpu_custom_call" | custom-call | tf_op jit(solution)/shard_map/pallas_call | solution.py:654
  (3 shorter events, 0.0 us)
Async XLA Ops:
  3.6 5.9 %collective-permute-start.2 = (f32[136,128]{1,0:T(8,128)S(1)}, f32[136,128]{1,0:T(8,128)S(1)}, u32[]{:S(2)}, u32[]{:S(2)}) collective-permute-start(f32[136,128]{1,0:T(8,128)S(1)} %get-tuple-element.32), channel_id=1, source_target_pairs={{0,3},{1,0},{2,1},{3,2},{4,7},{5,4},{6,5},{7,6},{8,11},{9,8},{10,9... | collective-permute-start | bytes 208904 | tf_op jit(solution)/shard_map/ppermute | solution.py:712
  4.3 5.2 %collective-permute-start = (f32[136,128]{1,0:T(8,128)S(1)}, f32[136,128]{1,0:T(8,128)S(1)}, u32[]{:S(2)}, u32[]{:S(2)}) collective-permute-start(f32[136,128]{1,0:T(8,128)S(1)} %get-tuple-element.25.own_ref), channel_id=1, source_target_pairs={{0,1},{1,2},{2,3},{3,0},{4,5},{5,6},{6,7},{7,4},{8,9},{9,10},{10,1... | collective-permute-start | bytes 208904 | tf_op jit(solution)/shard_map/ppermute | solution.py:712
  5.4 4.1 %collective-permute-start.1 = (f32[104,128]{1,0:T(8,128)S(1)}, f32[104,128]{1,0:T(8,128)S(1)}, u32[]{:S(2)}, u32[]{:S(2)}) collective-permute-start(f32[104,128]{1,0:T(8,128)S(1)} %get-tuple-element.31), channel_id=1, source_target_pairs={{0,2},{1,3},{2,0},{3,1},{4,6},{5,7},{6,4},{7,5},{8,10},{9,11},{10,... | collective-permute-start | bytes 159752 | tf_op jit(solution)/shard_map/ppermute | solution.py:712
  10.1 4.4 %collective-permute-start.3 = (f32[104,128]{1,0:T(8,128)S(1)}, f32[104,128]{1,0:T(8,128)S(1)}, u32[]{:S(2)}, u32[]{:S(2)}) collective-permute-start(f32[104,128]{1,0:T(8,128)S(1)} %get-tuple-element.35), channel_id=1, source_target_pairs={{0,4},{4,0},{1,5},{5,1},{2,6},{6,2},{3,7},{7,3},{8,12},{12,8},{9,1... | collective-permute-start | bytes 159752 | tf_op jit(solution)/shard_map/ppermute | solution.py:677
  14.7 3.7 %collective-permute-start.4 = (f32[136,128]{1,0:T(8,128)S(1)}, f32[136,128]{1,0:T(8,128)S(1)}, u32[]{:S(2)}, u32[]{:S(2)}) collective-permute-start(f32[136,128]{1,0:T(8,128)S(1)} %get-tuple-element.41), channel_id=1, source_target_pairs={{0,8},{16,24},{8,0},{24,16},{1,9},{17,25},{9,1},{25,17},{2,10},{18... | collective-permute-start | bytes 208904 | tf_op jit(solution)/shard_map/ppermute | solution.py:677
  14.8 4.0 %collective-permute-start.5 = (f32[136,128]{1,0:T(8,128)S(1)}, f32[136,128]{1,0:T(8,128)S(1)}, u32[]{:S(2)}, u32[]{:S(2)}) collective-permute-start(f32[136,128]{1,0:T(8,128)S(1)} %get-tuple-element.42), channel_id=1, source_target_pairs={{8,16},{9,17},{10,18},{11,19},{16,8},{17,9},{18,10},{19,11},{0,1},... | collective-permute-start | bytes 208904 | tf_op jit(solution)/shard_map/ppermute | solution.py:677
  19.4 5.1 %collective-permute-start.6 = (f32[32,384]{1,0:T(8,128)S(1)}, f32[32,384]{1,0:T(8,128)S(1)}, u32[]{:S(2)}, u32[]{:S(2)}) collective-permute-start(f32[32,384]{1,0:T(8,128)S(1)} %get-tuple-element.44), channel_id=1, source_target_pairs={{0,1},{1,2},{2,3},{3,0},{4,5},{5,6},{6,7},{7,4},{8,9},{9,10},{10,1... | collective-permute-start | bytes 147464 | tf_op jit(solution)/shard_map/ppermute | solution.py:737
  21.7 4.6 %collective-permute-start.7 = (f32[32,384]{1,0:T(8,128)S(1)}, f32[32,384]{1,0:T(8,128)S(1)}, u32[]{:S(2)}, u32[]{:S(2)}) collective-permute-start(f32[32,384]{1,0:T(8,128)S(1)} %get-tuple-element.45), channel_id=1, source_target_pairs={{0,2},{1,3},{2,0},{3,1},{4,6},{5,7},{6,4},{7,5},{8,10},{9,11},{10,... | collective-permute-start | bytes 147464 | tf_op jit(solution)/shard_map/ppermute | solution.py:737
  23.7 3.5 %collective-permute-start.8 = (f32[32,384]{1,0:T(8,128)S(1)}, f32[32,384]{1,0:T(8,128)S(1)}, u32[]{:S(2)}, u32[]{:S(2)}) collective-permute-start(f32[32,384]{1,0:T(8,128)S(1)} %get-tuple-element.46), channel_id=1, source_target_pairs={{0,3},{1,0},{2,1},{3,2},{4,7},{5,4},{6,5},{7,6},{8,11},{9,8},{10,9... | collective-permute-start | bytes 147464 | tf_op jit(solution)/shard_map/ppermute | solution.py:737
